TPU v7x, 128 devices: a whole 4x4x4 slice. The times are simulated.
128 devices in a mesh: src: 16 (over x, z_lo, core), freq: 8 (over y, z_hi).
Axes of the slice: x: 4, y: 4, z: 4 (z_hi: 2, z_lo: 2; z = z_hi * 2 + z_lo), core: 2. Of those that a mesh axis runs over, the one named last changes fastest.
Arguments:
- receivers: bfloat16 [8, 16, 2, 256, 512], P('freq', 'src'), may hold values from -6 to 6
- data: bfloat16 [8, 2, 8192, 2048], P('freq', None, None, 'src'), may hold values from -0.046875 to 0.046875
- block_of_slot: int32 [16], replicated, may hold values from 0 to 15, each once
- receiver_order: int32 [256], replicated, may hold values from 0 to 255, each once
Outputs:
- traces: bfloat16 [256, 2048, 256], P('freq', 'src')
Inputs may be any that keep to these rules, and one draw needn't show every extreme that they name: `block_of_slot`: each of the 16 bounce blocks is held in exactly one slot. `receiver_order`: each receiver appears in exactly one trace row.
All inputs are finite; a program needn't handle non-finite values.
Results may differ from a plain program's by a relative error of at most 0.0049.
Values may be sent and summed in bfloat16 or wider, within the bound.
A program may use at most 64 MiB of HBM per device.

v0:
```python
import math

import jax
import jax.numpy as jnp
from jax import lax
from jax.sharding import PartitionSpec as P

NT = 256


def spread(x, axis, root):
    mine = lax.axis_index(axis) == root
    return lax.psum(jnp.where(mine, x, jnp.zeros_like(x)), axis)


def multiply(acc, piece, block, data):
    width = piece.shape[3]
    rows = lax.dynamic_slice_in_dim(data, block * width, width, 2)
    g_re, g_im = (piece[:, 0], piece[:, 1])
    d_re, d_im = (rows[:, 0], rows[:, 1])
    real = jnp.einsum("frk,fks->frs", g_re, d_re, preferred_element_type=jnp.float32) - jnp.einsum(
        "frk,fks->frs", g_im, d_im, preferred_element_type=jnp.float32
    )
    imag = jnp.einsum("frk,fks->frs", g_re, d_im, preferred_element_type=jnp.float32) + jnp.einsum(
        "frk,fks->frs", g_im, d_re, preferred_element_type=jnp.float32
    )
    return acc + jnp.stack([real, imag], 1)


def transform(moved):
    high = lax.Precision.HIGHEST
    count = moved.shape[0]
    spectra = moved.astype(jnp.float32)
    times = jnp.arange(NT, dtype=jnp.int32)
    bins = (2 * jnp.arange(count, dtype=jnp.int32) + 1) * (NT // (4 * count))
    phase = bins[:, None] * times[None, :] % NT
    angle = phase.astype(jnp.float32) * (2.0 * math.pi / NT)
    cosine = jnp.cos(angle)
    sine = jnp.sin(angle)
    value = jnp.einsum("frs,ft->rst", spectra[:, 0], cosine, precision=high) - jnp.einsum(
        "frs,ft->rst", spectra[:, 1], sine, precision=high
    )
    return (value * count ** (-0.5)).astype(jnp.bfloat16)


def body(receivers, data, block_of_slot, receiver_order):
    slots_here = receivers.shape[1]
    start = jnp.zeros((receivers.shape[0], 2, receivers.shape[3], data.shape[3]), jnp.float32)
    total = slots_here * lax.axis_size("src")

    def turn(slot, acc):
        holder = slot // slots_here
        local = lax.dynamic_index_in_dim(receivers, slot % slots_here, 1, keepdims=False)
        shared = spread(local, "src", holder)
        return multiply(acc, shared, block_of_slot[slot], data)

    acc = lax.fori_loop(0, total, turn, start)
    spectra = acc.astype(jnp.bfloat16)
    ordered = jnp.take(spectra, receiver_order, axis=2)
    return transform(lax.all_to_all(ordered, "freq", split_axis=2, concat_axis=0, tiled=True))


def solution(mesh):
    placed = (P("freq", "src", None, None, None), P("freq", None, None, "src"), P(), P())
    return jax.shard_map(
        body, mesh=mesh, in_specs=placed, out_specs=P("freq", "src", None), check_vma=False
    )
```

profile of v0, /device:TPU:0, one launch (start us, length us, event | category | flops | bytes accessed | tf_op | source)
XLA Modules:
  0.0 2081.3 jit_solution(855906001196763200)
XLA Ops:
  7.9 2045.1 %while.16 = (s32[]{:T(128)}, f32[1,2,256,128]{3,2,1,0:T(8,128)S(1)}, bf16[1,1,2,256,512]{4,3,2,1,0:T(8,128)(2,1)}, s32[16]{0:T(128)}, bf16[1,2,8192,128]{3,2,1,0...) while((s32[]{:T(128)}, ...), condition=%wide.region_2.3_spmd.clone, body=%wide.region_0.2_spmd.clone.sunk | while | flops 135004160 | bytes 7340343 | solution.py:57
  8.0 1.9 select_bitcast_fusion.2
  9.9 1.3 dynamic_slice.27
  11.9 120.5 %all-reduce.2.cloned.1.call-done = bf16[1,2,256,512]{3,2,1,0:T(8,128)(2,1)} async-done(((bf16[1,2,256,512]{3,2,1,0:T(8,128)(2,1)}), bf16[1,2,256,512]{3,2,1,0:T(8,128)(2,1)}) %all-reduce.2.cloned.1.call-update) | async-done | bytes 524304 | tf_op jit(solution)/shard_map/while/body/eval_jaxpr/psum | solution.py:13
  134.8 1.2 fusion.37
  136.0 1.2 fusion.35
  138.3 1.3 dynamic_slice.27
  140.3 120.0 %all-reduce.2.cloned.1.call-done = bf16[1,2,256,512]{3,2,1,0:T(8,128)(2,1)} async-done(((bf16[1,2,256,512]{3,2,1,0:T(8,128)(2,1)}), bf16[1,2,256,512]{3,2,1,0:T(8,128)(2,1)}) %all-reduce.2.cloned.1.call-update) | async-done | bytes 524304 | tf_op jit(solution)/shard_map/while/body/eval_jaxpr/psum | solution.py:13
  261.5 1.2 fusion.34
  263.9 1.2 fusion.35
  266.2 1.3 dynamic_slice.27
  268.1 120.0 %all-reduce.2.cloned.1.call-done = bf16[1,2,256,512]{3,2,1,0:T(8,128)(2,1)} async-done(((bf16[1,2,256,512]{3,2,1,0:T(8,128)(2,1)}), bf16[1,2,256,512]{3,2,1,0:T(8,128)(2,1)}) %all-reduce.2.cloned.1.call-update) | async-done | bytes 524304 | tf_op jit(solution)/shard_map/while/body/eval_jaxpr/psum | solution.py:13
  389.4 1.2 fusion.34
  390.6 1.2 fusion.37
  391.8 1.2 fusion.35
  394.0 1.3 dynamic_slice.27
  396.0 119.7 %all-reduce.2.cloned.1.call-done = bf16[1,2,256,512]{3,2,1,0:T(8,128)(2,1)} async-done(((bf16[1,2,256,512]{3,2,1,0:T(8,128)(2,1)}), bf16[1,2,256,512]{3,2,1,0:T(8,128)(2,1)}) %all-reduce.2.cloned.1.call-update) | async-done | bytes 524304 | tf_op jit(solution)/shard_map/while/body/eval_jaxpr/psum | solution.py:13
  518.1 1.2 fusion.37
  521.6 1.3 dynamic_slice.27
  523.6 119.7 %all-reduce.2.cloned.1.call-done = bf16[1,2,256,512]{3,2,1,0:T(8,128)(2,1)} async-done(((bf16[1,2,256,512]{3,2,1,0:T(8,128)(2,1)}), bf16[1,2,256,512]{3,2,1,0:T(8,128)(2,1)}) %all-reduce.2.cloned.1.call-update) | async-done | bytes 524304 | tf_op jit(solution)/shard_map/while/body/eval_jaxpr/psum | solution.py:13
  645.7 1.2 fusion.37
  649.2 1.3 dynamic_slice.27
  651.1 119.7 %all-reduce.2.cloned.1.call-done = bf16[1,2,256,512]{3,2,1,0:T(8,128)(2,1)} async-done(((bf16[1,2,256,512]{3,2,1,0:T(8,128)(2,1)}), bf16[1,2,256,512]{3,2,1,0:T(8,128)(2,1)}) %all-reduce.2.cloned.1.call-update) | async-done | bytes 524304 | tf_op jit(solution)/shard_map/while/body/eval_jaxpr/psum | solution.py:13
  774.5 1.2 fusion.35
  776.7 1.3 dynamic_slice.27
  778.7 120.0 %all-reduce.2.cloned.1.call-done = bf16[1,2,256,512]{3,2,1,0:T(8,128)(2,1)} async-done(((bf16[1,2,256,512]{3,2,1,0:T(8,128)(2,1)}), bf16[1,2,256,512]{3,2,1,0:T(8,128)(2,1)}) %all-reduce.2.cloned.1.call-update) | async-done | bytes 524304 | tf_op jit(solution)/shard_map/while/body/eval_jaxpr/psum | solution.py:13
  900.0 1.2 fusion.34
  901.2 1.2 fusion.37
  902.4 1.2 fusion.35
  904.6 1.3 dynamic_slice.27
  906.6 120.0 %all-reduce.2.cloned.1.call-done = bf16[1,2,256,512]{3,2,1,0:T(8,128)(2,1)} async-done(((bf16[1,2,256,512]{3,2,1,0:T(8,128)(2,1)}), bf16[1,2,256,512]{3,2,1,0:T(8,128)(2,1)}) %all-reduce.2.cloned.1.call-update) | async-done | bytes 524304 | tf_op jit(solution)/shard_map/while/body/eval_jaxpr/psum | solution.py:13
  1029.0 1.2 fusion.37
  1030.2 1.2 fusion.35
  1032.5 1.3 dynamic_slice.27
  1034.5 120.0 %all-reduce.2.cloned.1.call-done = bf16[1,2,256,512]{3,2,1,0:T(8,128)(2,1)} async-done(((bf16[1,2,256,512]{3,2,1,0:T(8,128)(2,1)}), bf16[1,2,256,512]{3,2,1,0:T(8,128)(2,1)}) %all-reduce.2.cloned.1.call-update) | async-done | bytes 524304 | tf_op jit(solution)/shard_map/while/body/eval_jaxpr/psum | solution.py:13
  1156.9 1.2 fusion.37
  1160.4 1.3 dynamic_slice.27
  1162.3 119.7 %all-reduce.2.cloned.1.call-done = bf16[1,2,256,512]{3,2,1,0:T(8,128)(2,1)} async-done(((bf16[1,2,256,512]{3,2,1,0:T(8,128)(2,1)}), bf16[1,2,256,512]{3,2,1,0:T(8,128)(2,1)}) %all-reduce.2.cloned.1.call-update) | async-done | bytes 524304 | tf_op jit(solution)/shard_map/while/body/eval_jaxpr/psum | solution.py:13
  1284.5 1.2 fusion.37
  1285.7 1.2 fusion.35
  1287.9 1.3 dynamic_slice.27
  1289.9 120.0 %all-reduce.2.cloned.1.call-done = bf16[1,2,256,512]{3,2,1,0:T(8,128)(2,1)} async-done(((bf16[1,2,256,512]{3,2,1,0:T(8,128)(2,1)}), bf16[1,2,256,512]{3,2,1,0:T(8,128)(2,1)}) %all-reduce.2.cloned.1.call-update) | async-done | bytes 524304 | tf_op jit(solution)/shard_map/while/body/eval_jaxpr/psum | solution.py:13
  1412.3 1.2 fusion.37
  1415.8 1.3 dynamic_slice.27
  1417.8 119.7 %all-reduce.2.cloned.1.call-done = bf16[1,2,256,512]{3,2,1,0:T(8,128)(2,1)} async-done(((bf16[1,2,256,512]{3,2,1,0:T(8,128)(2,1)}), bf16[1,2,256,512]{3,2,1,0:T(8,128)(2,1)}) %all-reduce.2.cloned.1.call-update) | async-done | bytes 524304 | tf_op jit(solution)/shard_map/while/body/eval_jaxpr/psum | solution.py:13
  1539.9 1.2 fusion.37
  1541.1 1.2 fusion.35
  1543.4 1.3 dynamic_slice.27
  1545.3 120.0 %all-reduce.2.cloned.1.call-done = bf16[1,2,256,512]{3,2,1,0:T(8,128)(2,1)} async-done(((bf16[1,2,256,512]{3,2,1,0:T(8,128)(2,1)}), bf16[1,2,256,512]{3,2,1,0:T(8,128)(2,1)}) %all-reduce.2.cloned.1.call-update) | async-done | bytes 524304 | tf_op jit(solution)/shard_map/while/body/eval_jaxpr/psum | solution.py:13
  1666.6 1.2 fusion.34
  1669.0 1.2 fusion.35
  1671.2 1.3 dynamic_slice.27
  1673.2 119.7 %all-reduce.2.cloned.1.call-done = bf16[1,2,256,512]{3,2,1,0:T(8,128)(2,1)} async-done(((bf16[1,2,256,512]{3,2,1,0:T(8,128)(2,1)}), bf16[1,2,256,512]{3,2,1,0:T(8,128)(2,1)}) %all-reduce.2.cloned.1.call-update) | async-done | bytes 524304 | tf_op jit(solution)/shard_map/while/body/eval_jaxpr/psum | solution.py:13
  1795.4 1.2 fusion.37
  1798.8 1.3 dynamic_slice.27
  1800.8 119.7 %all-reduce.2.cloned.1.call-done = bf16[1,2,256,512]{3,2,1,0:T(8,128)(2,1)} async-done(((bf16[1,2,256,512]{3,2,1,0:T(8,128)(2,1)}), bf16[1,2,256,512]{3,2,1,0:T(8,128)(2,1)}) %all-reduce.2.cloned.1.call-update) | async-done | bytes 524304 | tf_op jit(solution)/shard_map/while/body/eval_jaxpr/psum | solution.py:13
  1922.9 1.2 fusion.37
  1926.4 1.3 dynamic_slice.27
  1928.3 119.7 %all-reduce.2.cloned.1.call-done = bf16[1,2,256,512]{3,2,1,0:T(8,128)(2,1)} async-done(((bf16[1,2,256,512]{3,2,1,0:T(8,128)(2,1)}), bf16[1,2,256,512]{3,2,1,0:T(8,128)(2,1)}) %all-reduce.2.cloned.1.call-update) | async-done | bytes 524304 | tf_op jit(solution)/shard_map/while/body/eval_jaxpr/psum | solution.py:13
  2050.5 1.2 fusion.37
  2055.1 6.5 all-to-all-start
  2061.6 7.9 all-to-all-done
  2069.6 1.9 fusion.9
  2071.5 3.3 multiply_convert_fusion
  (111 shorter events, 63.7 us)
Async XLA Ops:
  7.9 124.5 %all-reduce.2.cloned.1.call-start = ((), (), s32[]{:S(2)}) async-start(), calls=%async_computation.1 | async-start | bytes 1048576 | tf_op jit(solution)/shard_map/while/body/eval_jaxpr/psum | solution.py:13
  137.3 123.0 %all-reduce.2.cloned.1.call-start = ((), (), s32[]{:S(2)}) async-start(), calls=%async_computation.1 | async-start | bytes 1048576 | tf_op jit(solution)/shard_map/while/body/eval_jaxpr/psum | solution.py:13
  265.2 123.0 %all-reduce.2.cloned.1.call-start = ((), (), s32[]{:S(2)}) async-start(), calls=%async_computation.1 | async-start | bytes 1048576 | tf_op jit(solution)/shard_map/while/body/eval_jaxpr/psum | solution.py:13
  393.1 122.6 %all-reduce.2.cloned.1.call-start = ((), (), s32[]{:S(2)}) async-start(), calls=%async_computation.1 | async-start | bytes 1048576 | tf_op jit(solution)/shard_map/while/body/eval_jaxpr/psum | solution.py:13
  520.7 122.6 %all-reduce.2.cloned.1.call-start = ((), (), s32[]{:S(2)}) async-start(), calls=%async_computation.1 | async-start | bytes 1048576 | tf_op jit(solution)/shard_map/while/body/eval_jaxpr/psum | solution.py:13
  648.2 122.6 %all-reduce.2.cloned.1.call-start = ((), (), s32[]{:S(2)}) async-start(), calls=%async_computation.1 | async-start | bytes 1048576 | tf_op jit(solution)/shard_map/while/body/eval_jaxpr/psum | solution.py:13
  775.8 123.0 %all-reduce.2.cloned.1.call-start = ((), (), s32[]{:S(2)}) async-start(), calls=%async_computation.1 | async-start | bytes 1048576 | tf_op jit(solution)/shard_map/while/body/eval_jaxpr/psum | solution.py:13
  903.7 123.0 %all-reduce.2.cloned.1.call-start = ((), (), s32[]{:S(2)}) async-start(), calls=%async_computation.1 | async-start | bytes 1048576 | tf_op jit(solution)/shard_map/while/body/eval_jaxpr/psum | solution.py:13
  1031.5 123.0 %all-reduce.2.cloned.1.call-start = ((), (), s32[]{:S(2)}) async-start(), calls=%async_computation.1 | async-start | bytes 1048576 | tf_op jit(solution)/shard_map/while/body/eval_jaxpr/psum | solution.py:13
  1159.4 122.6 %all-reduce.2.cloned.1.call-start = ((), (), s32[]{:S(2)}) async-start(), calls=%async_computation.1 | async-start | bytes 1048576 | tf_op jit(solution)/shard_map/while/body/eval_jaxpr/psum | solution.py:13
  1287.0 123.0 %all-reduce.2.cloned.1.call-start = ((), (), s32[]{:S(2)}) async-start(), calls=%async_computation.1 | async-start | bytes 1048576 | tf_op jit(solution)/shard_map/while/body/eval_jaxpr/psum | solution.py:13
  1414.9 122.6 %all-reduce.2.cloned.1.call-start = ((), (), s32[]{:S(2)}) async-start(), calls=%async_computation.1 | async-start | bytes 1048576 | tf_op jit(solution)/shard_map/while/body/eval_jaxpr/psum | solution.py:13
  1542.4 123.0 %all-reduce.2.cloned.1.call-start = ((), (), s32[]{:S(2)}) async-start(), calls=%async_computation.1 | async-start | bytes 1048576 | tf_op jit(solution)/shard_map/while/body/eval_jaxpr/psum | solution.py:13
  1670.3 122.6 %all-reduce.2.cloned.1.call-start = ((), (), s32[]{:S(2)}) async-start(), calls=%async_computation.1 | async-start | bytes 1048576 | tf_op jit(solution)/shard_map/while/body/eval_jaxpr/psum | solution.py:13
  1797.9 122.6 %all-reduce.2.cloned.1.call-start = ((), (), s32[]{:S(2)}) async-start(), calls=%async_computation.1 | async-start | bytes 1048576 | tf_op jit(solution)/shard_map/while/body/eval_jaxpr/psum | solution.py:13
  1925.4 122.6 %all-reduce.2.cloned.1.call-start = ((), (), s32[]{:S(2)}) async-start(), calls=%async_computation.1 | async-start | bytes 1048576 | tf_op jit(solution)/shard_map/while/body/eval_jaxpr/psum | solution.py:13
  2055.1 14.5 all-to-all-start
Sparse Core Ops, SparseCore 0:
  11.2 121.1 all-reduce.1
  140.6 119.6 all-reduce.1
  268.5 119.6 all-reduce.1
  396.1 119.6 all-reduce.1
  523.6 119.6 all-reduce.1
  651.2 119.6 all-reduce.1
  779.1 119.6 all-reduce.1
  907.0 119.6 all-reduce.1
  1034.8 119.6 all-reduce.1
  1162.4 119.6 all-reduce.1
  1290.3 119.6 all-reduce.1
  1417.8 119.6 all-reduce.1
  1545.7 119.6 all-reduce.1
  1673.3 119.6 all-reduce.1
  1800.8 119.6 all-reduce.1
  1928.4 119.6 all-reduce.1
where the time goes:
time: 2080 us
  waiting for transfers between devices  1930 us (93%)
  matrix products  81.9 us (4%)
  local copies, waits for them, and re-layouts  22 us (1%)
    psum x16, waiting for transfers between devices, spread(): return lax.psum(jnp.where(mine, x, jnp.zeros_like(x)), axis)  1920 us
  transfers between devices with their start and end apart: 17, of which 17 were waited for; matrix products, arithmetic and copies ran while one was open for 1% of the time, Pallas kernels for 0%

commit v1 on v0

v1 whole, which is shorter than its diff:
```python
import math

import jax
import jax.numpy as jnp
import numpy as np
from jax import lax
from jax.sharding import PartitionSpec as P

NT = 256


def tables(count):
    times = np.arange(NT)
    bins = (2 * np.arange(count) + 1) * (NT // (4 * count))
    angle = (bins[:, None] * times[None, :] % NT) * (2.0 * math.pi / NT)
    full = np.stack([np.cos(angle), -np.sin(angle)], 1) * count ** (-0.5)
    return full.astype(np.float32)


def body(receivers, data, block_of_slot, receiver_order):
    width = receivers.shape[4]
    blocks = lax.all_gather(receivers[0], "src", axis=0, tiled=True)
    slots = blocks.shape[0]
    rows = data[0].reshape(2, slots, width, data.shape[3])
    slot_of_block = jnp.argsort(block_of_slot)
    moved = jnp.take(blocks, slot_of_block, axis=0)
    acc = jnp.einsum("jcrk,djks->cdrs", moved, rows, preferred_element_type=jnp.float32)
    spectra = jnp.stack([acc[0, 0] - acc[1, 1], acc[0, 1] + acc[1, 0]], 0).astype(jnp.bfloat16)
    ordered = jnp.take(spectra, receiver_order, axis=1)[None]
    got = lax.all_to_all(ordered, "freq", split_axis=2, concat_axis=0, tiled=True)
    table = jnp.asarray(tables(got.shape[0]))
    high = table.astype(jnp.bfloat16)
    low = (table - high.astype(jnp.float32)).astype(jnp.bfloat16)
    value = jnp.einsum("fcrs,fct->rst", got, high, preferred_element_type=jnp.float32)
    value = value + jnp.einsum("fcrs,fct->rst", got, low, preferred_element_type=jnp.float32)
    return value.astype(jnp.bfloat16)


def solution(mesh):
    placed = (P("freq", "src", None, None, None), P("freq", None, None, "src"), P(), P())
    return jax.shard_map(
        body, mesh=mesh, in_specs=placed, out_specs=P("freq", "src", None), check_vma=False
    )
```

time: 2080 us -> 105 us (0.05)
  waiting for transfers between devices: 1930 us -> 53.8 us
  matrix products: 81.9 us -> 9.82 us
    psum x16 -> x0, waiting for transfers between devices: 1920 us -> none  [spread(): return lax.psum(jnp.where(mine, x, jnp.zeros_like(x)), axis)]
    dot_general x66 -> x3, matrix products: 81.9 us -> 9.82 us  [the longest x1 6.97 us: body(): jnp.einsum('jcrk,djks->cdrs', moved, rows, preferred_element_type=jnp.flo...]
    all_gather x0 -> x1, waiting for transfers between devices: none -> 53.1 us  [body(): blocks = lax.all_gather(receivers[0], 'src', axis=0, tiled=True)]
    dynamic_slice x16 -> x0, local copies, waits for them, and re-layouts: 20.9 us -> none  [turn(): return multiply(acc, shared, block_of_slot[slot], data)]
  transfers between devices with their start and end apart: 17 -> 1, of which waited for: 17 -> 1; matrix products, arithmetic and copies ran while one was open for 1% -> 3% of each run, Pallas kernels for 0% -> 0%
where the time goes in v1:
time: 105 us; the launch traced here: 104 us
  waiting for transfers between devices  53.8 us (51%)
  blocking collectives  14.4 us (14%)
  between operations  13.5 us (13%)
  matrix products  9.82 us (9%)
  local copies, waits for them, and re-layouts  9.21 us (9%)
  other arithmetic  3.68 us (4%)
    all_gather x1, waiting for transfers between devices, body(): blocks = lax.all_gather(receivers[0], 'src', axis=0, tiled=True)  53.1 us
    all_to_all x1, blocking collectives, body(): lax.all_to_all(ordered, 'freq', split_axis=2, concat_axis=0, tiled=True)  14.4 us
    gather x1, local copies, waits for them, and re-layouts, body(): moved = jnp.take(blocks, slot_of_block, axis=0)  8.13 us
    dot_general x1, matrix products, body(): jnp.einsum('jcrk,djks->cdrs', moved, rows, preferred_element_type=jnp.flo...  6.97 us
  transfers between devices with their start and end apart: 1, of which 1 were waited for; matrix products, arithmetic and copies ran while one was open for 3% of the time, Pallas kernels for 0%

profile of v1, /device:TPU:0, one launch (start us, length us, event | category | flops | bytes accessed | tf_op | source)
XLA Modules:
  0.0 104.4 jit_solution(16391787386407409647)
XLA Ops:
  6.5 0.0 all-gather.3.cloned.1.call-start
  6.5 0.7 all-gather.3.cloned.1.call-update
  7.3 1.9 %sort.17 = (s32[16]{0:T(128)}, s32[16]{0:T(128)S(1)}) sort(s32[16]{0:T(128)} %param.7, s32[16]{0:T(128)S(1)} %iota.4), dimensions={0}, to_apply=%region_0.0 | sort | flops 64 | bytes 256 | tf_op jit(solution)/shard_map/jit(argsort)/sort | solution.py:25
  9.2 0.7 compare_select_fusion
  9.9 0.7 compare_and_fusion.1
  10.6 53.1 %all-gather.3.cloned.1.call-done = bf16[16,1,2,256,512]{4,3,2,1,0:T(8,128)(2,1)} async-done(((bf16[1,1,2,256,512]{4,3,2,1,0:T(8,128)(2,1)}), bf16[16,1,2,256,512]{4,3,2,1,0:T(8,128)(2,1)}) %all-gather.3.cloned.1.call-update) | async-done | bytes 8388624 | tf_op jit(solution)/shard_map/all_gather | solution.py:22
  63.7 8.1 %gather_fusion = bf16[16,2,256,512]{3,2,1,0:T(8,128)(2,1)} fusion(bf16[16,2,256,512]{3,2,1,0:T(8,128)(2,1)} %bitcast.46, s32[1024]{0:T(1024)S(1)} %pad_clamp_fusion.1), kind=kCustom, calls=%fused_computation | custom fusion | bytes 16777280 | tf_op jit(solution)/shard_map/jit(_take)/gather | solution.py:26
  71.8 0.0 copy-start
  71.8 0.0 copy-start.1
  71.8 7.0 %fusion.3 = f32[2,2,256,128]{3,2,1,0:T(8,128)S(1)} fusion(bf16[2,16,512,128,1]{3,2,1,0,4:T(8,128)(2,1)} %bitcast.49, bf16[16,2,256,512]{3,2,1,0:T(8,128)(2,1)} %gather_fusion, pred[16]{0:T(512)(128)(4,1)S(1)} %compare_and_fusion), kind=kOutput, calls=%fused_computation.7 | convolution fusion | flops 2151677952 | bytes 13107216 | tf_op jit(solution)/shard_map/jcrk,djks->cdrs/dot_general | solution.py:27
  78.8 0.1 copy.15
  79.0 0.9 gather_fusion.1
  79.9 0.3 fusion.11
  80.3 14.4 %all_to_all.18 = bf16[1,2,256,128]{3,1,0,2:T(2,128)(2,1)S(1)} all-to-all(bf16[1,2,256,128]{3,1,0,2:T(2,128)(2,1)S(1)} %fusion.11), channel_id=1, replica_groups=mesh['src'=16,'freq'=8] {'freq'}, dimensions={2} | all-to-all | bytes 262144 | tf_op jit(solution)/shard_map/all_to_all | solution.py:30
  94.7 0.0 copy-done
  94.7 0.8 fusion.9
  95.5 0.0 copy-done.1
  95.5 2.1 %fusion.2 = bf16[32,128,256]{2,1,0:T(8,128)(2,1)} fusion(f32[32,128,256,1]{2,1,3,0:T(8,128)S(1)} %fusion.9, bf16[8,2,256,1]{2,0,1,3:T(8,128)(2,1)S(1)} %copy-done.1, bf16[1,2,8,32,128]{4,1,3,2,0:T(2,128)(2,1)S(1)} %bitcast.48), kind=kOutput, calls=%fused_computation.6 | convolution fusion | flops 35651584 | bytes 6430720 | tf_op jit(solution)/shard_map/fcrs,fct->rst/dot_general | solution.py:35
  (7 shorter events, 0.1 us)
Async XLA Ops:
  6.5 57.1 %all-gather.3.cloned.1.call-start = ((), (), s32[]{:S(2)}) async-start(), calls=%async_computation.1 | async-start | bytes 8912896 | tf_op jit(solution)/shard_map/all_gather | solution.py:22
  71.8 22.9 %copy-start = (bf16[8,2,256,1]{2,0,1,3:T(8,128)(2,1)S(1)}, bf16[8,2,256,1]{2,0,1,3:T(8,128)(2,1)}, u32[]{:S(2)}) copy-start(bf16[8,2,256,1]{2,0,1,3:T(8,128)(2,1)} %constant.39) | copy-start | bytes 24580
  71.8 23.7 %copy-start.1 = (bf16[8,2,256,1]{2,0,1,3:T(8,128)(2,1)S(1)}, bf16[8,2,256,1]{2,0,1,3:T(8,128)(2,1)}, u32[]{:S(2)}) copy-start(bf16[8,2,256,1]{2,0,1,3:T(8,128)(2,1)} %constant.40) | copy-start | bytes 24580
Sparse Core Ops, SparseCore 0:
  9.0 54.5 all-gather.2

commit v2 on v1

v2 whole, which is shorter than its diff:
```python
import functools
import math

import jax
import jax.numpy as jnp
import numpy as np
from jax import lax
from jax.experimental import pallas as pl
from jax.experimental.pallas import tpu as pltpu
from jax.sharding import PartitionSpec as P

NT = 256
MESH = pl.DeviceIdType.MESH
CHUNK = 64

SENDS = {
    "xp": [(0, 0, 0, 4), (0, 0, 4, 4)]
    + [(-1, 0, k, 1) for k in range(4)]
    + [(0, 1, 1, 3), (0, 1, 4, 2), (0, 1, 6, 2)],
    "xm": [(0, 0, 4, 4), (0, 0, 0, 4)]
    + [(1, 0, 4 + k, 1) for k in range(4)]
    + [(0, 1, 4, 3), (0, 1, 2, 2), (0, 1, 0, 2)],
    "z": [(0, 0, 0, 4), (0, 0, 4, 4), (-1, 0, 0, 1), (1, 0, 7, 1)]
    + [(2, 0, 4 * (k % 2) + k // 2, 1) for k in range(8)],
    "c": [(0, 0, 0, 4), (0, 0, 4, 4)]
    + [(-1, 0, 0, 4), (1, 0, 4, 4), (0, 1, 0, 4)]
    + [(-1, 0, 4, 4), (1, 0, 0, 4), (0, 1, 4, 4)]
    + [(2, 0, 0, 4), (2, 0, 4, 4)]
    + [(-1, 1, 0, 4), (1, 1, 4, 4), (2, 1, 0, 2), (2, 1, 4, 2)]
    + [(-1, 1, 4, 2), (1, 1, 2, 2)]
    + [(2, 1, 2, 2), (2, 1, 6, 2)]
    + [(-1, 1, 6, 2), (1, 1, 0, 2)],
}
SHIFT = {"xp": (-1, 0, 0), "xm": (1, 0, 0), "z": (0, 1, 0), "c": (0, 0, 1)}
COUNT = {link: len(rows) for link, rows in SENDS.items()}


def tables(count):
    times = np.arange(NT)
    bins = (2 * np.arange(count) + 1) * (NT // (4 * count))
    angle = (bins[:, None] * times[None, :] % NT) * (2.0 * math.pi / NT)
    full = np.stack([np.cos(angle), -np.sin(angle)], 1) * count ** (-0.5)
    full = full.reshape(2 * count, NT).astype(np.float32)
    high = full.astype(jnp.bfloat16).astype(np.float32)
    low = (full - high).astype(jnp.bfloat16).astype(np.float32)
    return np.concatenate([high, low], 0)


def gather_kernel(
    freqs, block_ref, order_ref, own_hbm, data_hbm, out_ref,
    held, data, acc, perm, mix, outgoing, arrived,
    sx, rx, sf, rf, local,
):
    me = lax.axis_index("src")
    mine = lax.axis_index("freq")
    x, z, c = me // 4, (me // 2) % 2, me % 2
    depth = own_hbm.shape[1]
    rows = own_hbm.shape[0] // 2
    part = rows // freqs

    def slot(dx, dz, dc):
        return ((x + dx + 4) % 4) * 4 + ((z + dz) % 2) * 2 + (c + dc) % 2

    target = {"xp": slot(1, 0, 0), "xm": slot(-1, 0, 0), "z": slot(0, 1, 0), "c": slot(0, 0, 1)}
    first = {}
    at = 0
    for link in SENDS:
        first[link] = at
        at += COUNT[link]

    own_copy = pltpu.make_async_copy(own_hbm, held.at[me], local.at[0])
    data_copy = pltpu.make_async_copy(data_hbm, data, local.at[1])
    own_copy.start()
    data_copy.start()

    barrier = pltpu.get_barrier_semaphore()
    for link in SENDS:
        pl.semaphore_signal(barrier, inc=1, device_id={"src": target[link]}, device_id_type=MESH)
    for d in range(1, freqs):
        pl.semaphore_signal(barrier, inc=1, device_id={"freq": (mine + d) % freqs}, device_id_type=MESH)
    pl.semaphore_wait(barrier, len(SENDS) + freqs - 1)

    def copy(link, k, received=False):
        dx, dz, low, count = SENDS[link][k]
        dc = 0
        if received:
            sx_, sz_, dc = SHIFT[link]
            dx, dz = dx + sx_, dz + sz_
        piece = held.at[slot(dx, dz, dc), pl.ds(low * CHUNK, count * CHUNK)]
        return pltpu.make_async_remote_copy(
            src_ref=piece,
            dst_ref=piece,
            send_sem=sx.at[first[link] + k],
            recv_sem=rx.at[first[link] + k],
            device_id={"src": target[link]},
            device_id_type=MESH,
        )

    def send(link, *which):
        for k in which:
            copy(link, k).start()

    def wait(link, *which):
        for k in which:
            copy(link, k, True).wait_recv()

    def product(dx, dz, dc, low, count, fresh=False):
        j = slot(dx, dz, dc)
        block = block_ref[j]
        right = jnp.concatenate([data[0, block], data[1, block]], 1)
        span = pl.ds(low * CHUNK, count * CHUNK)
        value = jnp.dot(held[j, span, :], right, preferred_element_type=jnp.float32)
        if fresh:
            acc[span, :] = value
        else:
            acc[span, :] += value

    own_copy.wait()
    send("xp", 0)
    send("xm", 0)
    send("z", 0)
    send("xp", 1)
    send("xm", 1)
    send("z", 1)
    send("c", 0, 1)

    ids = lax.broadcasted_iota(jnp.int32, (rows, rows), 0)
    chosen = jnp.where(ids == order_ref[...], 1.0, 0.0).astype(jnp.float32)
    perm[...] = chosen.T.astype(jnp.bfloat16)
    n = lax.broadcasted_iota(jnp.int32, (2 * rows, 1), 0)
    source = (n % 2) * rows + ((n // 2) % freqs) * part + n // (2 * freqs)
    m = lax.broadcasted_iota(jnp.int32, (2 * rows, 2 * rows), 1)
    mix[...] = jnp.where(m == source, 1.0, 0.0).astype(jnp.bfloat16)

    data_copy.wait()
    product(0, 0, 0, 0, 8, fresh=True)
    wait("c", 0, 1)
    product(0, 0, 1, 0, 8)

    wait("xp", 0)
    send("xp", 2, 3, 4, 5)
    send("z", 2)
    send("c", 2)
    wait("xm", 0)
    send("xm", 2, 3, 4, 5)
    send("z", 3)
    send("c", 3)
    wait("z", 0)
    send("c", 4)
    product(-1, 0, 0, 0, 4)
    product(1, 0, 0, 4, 4)
    product(0, 1, 0, 0, 4)
    wait("c", 2, 3, 4)
    product(-1, 0, 1, 0, 4)
    product(1, 0, 1, 4, 4)
    product(0, 1, 1, 0, 4)

    wait("z", 1)
    send("xp", 6, 7, 8)
    send("xm", 6, 7, 8)
    wait("xp", 1)
    send("c", 5)
    wait("xm", 1)
    send("c", 6, 7)
    product(-1, 0, 0, 4, 4)
    product(1, 0, 0, 0, 4)
    product(0, 1, 0, 4, 4)
    wait("c", 5, 6, 7)
    product(-1, 0, 1, 4, 4)
    product(1, 0, 1, 0, 4)
    product(0, 1, 1, 4, 4)

    for k in range(4):
        wait("xp", 2 + k)
        send("z", 4 + 2 * k)
        wait("xm", 2 + k)
        send("z", 5 + 2 * k)
    send("c", 8, 9)
    product(2, 0, 0, 0, 8)
    wait("c", 8, 9)
    product(2, 0, 1, 0, 8)

    wait("z", 2, 3)
    wait("xp", 6)
    send("c", 10)
    wait("xm", 6)
    send("c", 11)
    wait("z", 4, 5, 6, 7)
    send("c", 12, 13)
    product(-1, 1, 0, 0, 4)
    product(1, 1, 0, 4, 4)
    wait("c", 10, 11)
    product(-1, 1, 1, 0, 4)
    product(1, 1, 1, 4, 4)

    wait("xp", 7)
    send("c", 14)
    wait("xm", 7)
    send("c", 15)
    product(-1, 1, 0, 4, 2)
    product(1, 1, 0, 2, 2)
    wait("z", 8, 10)
    send("c", 16)
    wait("z", 9, 11)
    send("c", 17)
    product(2, 1, 0, 0, 8)
    wait("c", 14, 15)
    product(-1, 1, 1, 4, 2)
    product(1, 1, 1, 2, 2)
    wait("c", 12, 13, 16, 17)
    product(2, 1, 1, 0, 8)

    wait("xp", 8)
    send("c", 18)
    wait("xm", 8)
    send("c", 19)
    product(-1, 1, 0, 6, 2)
    product(1, 1, 0, 0, 2)
    wait("c", 18, 19)
    product(-1, 1, 1, 6, 2)
    product(1, 1, 1, 0, 2)

    half = acc.shape[1] // 2
    real = acc[:rows, :half] - acc[rows:, half:]
    imag = acc[:rows, half:] + acc[rows:, :half]
    spectra = jnp.concatenate([real, imag], 1).astype(jnp.bfloat16)
    outgoing[...] = jnp.dot(perm[...], spectra, preferred_element_type=jnp.float32).astype(jnp.bfloat16)

    def share(d, received=False):
        peer = (mine + d) % freqs
        back = (mine - d + freqs) % freqs
        taken = outgoing.at[pl.ds(pl.multiple_of(peer * part, part), part)]
        landing = back if received else mine
        return pltpu.make_async_remote_copy(
            src_ref=taken,
            dst_ref=arrived.at[pl.ds(pl.multiple_of(landing * part, part), part)],
            send_sem=sf.at[d],
            recv_sem=rf.at[d],
            device_id={"freq": peer},
            device_id_type=MESH,
        )

    for d in range(1, freqs):
        share(d).start()
    here = pl.ds(pl.multiple_of(mine * part, part), part)
    keep = pltpu.make_async_copy(outgoing.at[here], arrived.at[here], local.at[0])
    keep.start()
    for link in SENDS:
        for k in range(COUNT[link]):
            copy(link, k).wait_send()
    keep.wait()
    for d in range(1, freqs):
        share(d, True).wait_recv()

    stacked = jnp.concatenate([arrived[:, :half], arrived[:, half:]], 0)
    mixed = jnp.dot(mix[...], stacked, preferred_element_type=jnp.float32)
    for g in range(2 * rows // half):
        span = pl.ds(g * half, half)
        out_ref[span, :] = mixed[g * half : (g + 1) * half, :].T.astype(jnp.bfloat16)
    for d in range(1, freqs):
        share(d).wait_send()


def transform_kernel(spectra_ref, table_ref, out_ref):
    step = pl.program_id(0)
    coefs = table_ref.shape[0] // 2
    each = spectra_ref.shape[1] // coefs
    high, low = table_ref[:coefs, :], table_ref[coefs:, :]
    full = jnp.concatenate([high] * each + [low] * each, 0)
    row = lax.broadcasted_iota(jnp.int32, full.shape, 0)
    right = jnp.where((row // coefs) % each == step, full, 0.0).astype(jnp.bfloat16)
    left = jnp.concatenate([spectra_ref[...], spectra_ref[...]], 1)
    value = jnp.dot(left, right, preferred_element_type=jnp.float32)
    out_ref[...] = value.astype(jnp.bfloat16).reshape(out_ref.shape)


def body(freqs, receivers, data, block_of_slot, receiver_order):
    rows, depth = receivers.shape[3], receivers.shape[4]
    points, width = data.shape[2], data.shape[3]
    slots = block_of_slot.shape[0]
    part = rows // freqs
    copies = sum(COUNT.values())
    moved = pl.pallas_call(
        functools.partial(gather_kernel, freqs),
        out_shape=jax.ShapeDtypeStruct((2 * rows, width), jnp.bfloat16),
        in_specs=[
            pl.BlockSpec(memory_space=pltpu.SMEM),
            pl.BlockSpec(memory_space=pltpu.VMEM),
            pl.BlockSpec(memory_space=pl.ANY),
            pl.BlockSpec(memory_space=pl.ANY),
        ],
        out_specs=pl.BlockSpec(memory_space=pltpu.VMEM),
        scratch_shapes=[
            pltpu.VMEM((slots, 2 * rows, depth), jnp.bfloat16),
            pltpu.VMEM((2, slots, depth, width), jnp.bfloat16),
            pltpu.VMEM((2 * rows, 2 * width), jnp.float32),
            pltpu.VMEM((rows, rows), jnp.bfloat16),
            pltpu.VMEM((2 * rows, 2 * rows), jnp.bfloat16),
            pltpu.VMEM((rows, 2 * width), jnp.bfloat16),
            pltpu.VMEM((rows, 2 * width), jnp.bfloat16),
            pltpu.SemaphoreType.DMA((copies,)),
            pltpu.SemaphoreType.DMA((copies,)),
            pltpu.SemaphoreType.DMA((freqs,)),
            pltpu.SemaphoreType.DMA((freqs,)),
            pltpu.SemaphoreType.DMA((2,)),
        ],
        compiler_params=pltpu.CompilerParams(
            collective_id=0, has_side_effects=True, vmem_limit_bytes=60 * 2**20
        ),
        name="gather_multiply_exchange",
    )(
        block_of_slot,
        receiver_order.reshape(1, rows),
        receivers.reshape(2 * rows, depth),
        data.reshape(2, slots, points // slots, width),
    )
    table = jnp.asarray(tables(freqs))
    each = width // (2 * freqs)
    groups = part // each
    traces = pl.pallas_call(
        transform_kernel,
        out_shape=jax.ShapeDtypeStruct((groups, each, width, NT), jnp.bfloat16),
        grid=(each,),
        in_specs=[
            pl.BlockSpec(moved.shape, lambda i: (0, 0)),
            pl.BlockSpec(table.shape, lambda i: (0, 0)),
        ],
        out_specs=pl.BlockSpec((groups, 1, width, NT), lambda i: (0, i, 0, 0)),
        name="transform",
    )(moved, table)
    return traces.reshape(part, width, NT)


def solution(mesh):
    placed = (P("freq", "src", None, None, None), P("freq", None, None, "src"), P(), P())
    return jax.shard_map(
        functools.partial(body, mesh.shape["freq"]),
        mesh=mesh,
        in_specs=placed,
        out_specs=P("freq", "src", None),
        check_vma=False,
    )
```

time: 105 us -> 53.2 us (0.51)
  waiting for transfers between devices: 53.8 us -> 0 us
  Pallas kernels: 0 us -> 52.3 us
  blocking collectives: 14.4 us -> 0 us
  between operations: 13.5 us -> 0.01 us
  matrix products: 9.82 us -> 0 us
  local copies, waits for them, and re-layouts: 9.21 us -> 0 us
  other arithmetic: 3.68 us -> 0 us
    all_gather x1 -> x0, waiting for transfers between devices: 53.1 us -> none  [body(): blocks = lax.all_gather(receivers[0], 'src', axis=0, tiled=True)]
    pallas_call x0 -> x2, Pallas kernels: none -> 52.3 us  [the longest x1 47.4 us: body(): pl.pallas_call(functools.partial(gather_kernel, freqs), out_shape=jax.Sha...]
    all_to_all x1 -> x0, blocking collectives: 14.4 us -> none  [body(): lax.all_to_all(ordered, 'freq', split_axis=2, concat_axis=0, tiled=True)]
    dot_general x3 -> x0, matrix products: 9.82 us -> none  [the longest x1 6.97 us: body(): jnp.einsum('jcrk,djks->cdrs', moved, rows, preferred_element_type=jnp.flo...]
    gather x2 -> x0, local copies, waits for them, and re-layouts: 9.06 us -> none  [the longest x1 8.13 us: body(): moved = jnp.take(blocks, slot_of_block, axis=0)]
    sort x1 -> x0, other arithmetic: 1.9 us -> none  [body(): slot_of_block = jnp.argsort(block_of_slot)]
  transfers between devices with their start and end apart: 1 -> 0, of which waited for: 1 -> 0; matrix products, arithmetic and copies ran while one was open for 3% -> 0% of each run, Pallas kernels for 0% -> 0%
where the time goes in v2:
time: 53.2 us; the launch traced here: 52.3 us
  Pallas kernels  52.3 us (98%)
    pallas_call x1, Pallas kernels, body(): pl.pallas_call(functools.partial(gather_kernel, freqs), out_shape=jax.Sha...  47.4 us
    pallas_call x1, Pallas kernels, body(): pl.pallas_call(transform_kernel, out_shape=jax.ShapeDtypeStruct((groups,...  4.96 us

profile of v2, /device:TPU:0, one launch (start us, length us, event | category | flops | bytes accessed | tf_op | source)
XLA Modules:
  0.0 52.3 jit_solution(2656382283287159759)
XLA Ops:
  0.0 47.4 %gather_multiply_exchange.1.spectra_ref = bf16[512,128]{1,0:T(8,128)(2,1)} custom-call(s32[16]{0:T(128)} %block_ref.1, s32[1,256]{1,0:T(1,128)} %bitcast.6, bf16[512,512]{1,0:T(8,128)(2,1)} %bitcast.5, bf16[2,16,512,128]{3,2,1,0:T(8,128)(2,1)} %bitcast.4), custom_call_target="tpu_custom_call" | custom-call | tf_op jit(solution)/shard_map/gather_multiply_exchange/pallas_call | solution.py:283
  47.4 5.0 %transform.1 = bf16[4,8,128,256]{3,2,1,0:T(8,128)(2,1)} custom-call(bf16[512,128]{1,0:T(8,128)(2,1)} %gather_multiply_exchange.1.spectra_ref, f32[32,256]{1,0:T(8,128)} %constant.2.clone.table_ref), custom_call_target="tpu_custom_call" | custom-call | tf_op jit(solution)/shard_map/transform/pallas_call | solution.py:320

commit v3 on v2

--- a/solution.py
+++ b/solution.py
@@ -49,7 +49,7 @@
 def gather_kernel(
     freqs, block_ref, order_ref, own_hbm, data_hbm, out_ref,
     held, data, acc, perm, mix, outgoing, arrived,
-    sx, rx, sf, rf, local,
+    sx, rx, sf, rf, local, known,
 ):
     me = lax.axis_index("src")
     mine = lax.axis_index("freq")
@@ -76,9 +76,20 @@
     barrier = pltpu.get_barrier_semaphore()
     for link in SENDS:
         pl.semaphore_signal(barrier, inc=1, device_id={"src": target[link]}, device_id_type=MESH)
-    for d in range(1, freqs):
-        pl.semaphore_signal(barrier, inc=1, device_id={"freq": (mine + d) % freqs}, device_id_type=MESH)
-    pl.semaphore_wait(barrier, len(SENDS) + freqs - 1)
+    after, before = {"freq": (mine + 2) % freqs}, {"freq": (mine + freqs - 2) % freqs}
+    inner, outer = {"src": target["z"]}, {"src": target["z"], "freq": mine + 1 - 2 * (mine % 2)}
+    for peer in (after, before, outer):
+        pl.semaphore_signal(barrier, inc=1, device_id=peer, device_id_type=MESH)
+    pl.semaphore_wait(barrier, len(SENDS) + 3)
+
+    rounds = ((before, inner), (before, after), (before,))
+
+    def tell(k):
+        for peer in rounds[k]:
+            pl.semaphore_signal(known.at[k], inc=1, device_id=peer, device_id_type=MESH)
+
+    def hear(k):
+        pl.semaphore_wait(known.at[k], len(rounds[k]))
 
     def copy(link, k, received=False):
         dx, dz, low, count = SENDS[link][k]
@@ -123,6 +134,7 @@
     send("xm", 1)
     send("z", 1)
     send("c", 0, 1)
+    tell(0)
 
     ids = lax.broadcasted_iota(jnp.int32, (rows, rows), 0)
     chosen = jnp.where(ids == order_ref[...], 1.0, 0.0).astype(jnp.float32)
@@ -150,6 +162,8 @@
     product(-1, 0, 0, 0, 4)
     product(1, 0, 0, 4, 4)
     product(0, 1, 0, 0, 4)
+    hear(0)
+    tell(1)
     wait("c", 2, 3, 4)
     product(-1, 0, 1, 0, 4)
     product(1, 0, 1, 4, 4)
@@ -165,7 +179,10 @@
     product(-1, 0, 0, 4, 4)
     product(1, 0, 0, 0, 4)
     product(0, 1, 0, 4, 4)
+    hear(1)
+    tell(2)
     wait("c", 5, 6, 7)
+    hear(2)
     product(-1, 0, 1, 4, 4)
     product(1, 0, 1, 0, 4)
     product(0, 1, 1, 4, 4)
@@ -262,16 +279,19 @@
 
 
 def transform_kernel(spectra_ref, table_ref, out_ref):
-    step = pl.program_id(0)
     coefs = table_ref.shape[0] // 2
     each = spectra_ref.shape[1] // coefs
+    groups, count, width, times = out_ref.shape
+    step = pl.program_id(0)
     high, low = table_ref[:coefs, :], table_ref[coefs:, :]
     full = jnp.concatenate([high] * each + [low] * each, 0)
     row = lax.broadcasted_iota(jnp.int32, full.shape, 0)
-    right = jnp.where((row // coefs) % each == step, full, 0.0).astype(jnp.bfloat16)
     left = jnp.concatenate([spectra_ref[...], spectra_ref[...]], 1)
-    value = jnp.dot(left, right, preferred_element_type=jnp.float32)
-    out_ref[...] = value.astype(jnp.bfloat16).reshape(out_ref.shape)
+    for u in range(count):
+        here = (row // coefs) % each == step * count + u
+        right = jnp.where(here, full, 0.0).astype(jnp.bfloat16)
+        value = jnp.dot(left, right, preferred_element_type=jnp.float32)
+        out_ref[:, u] = value.astype(jnp.bfloat16).reshape(groups, width, times)
 
 
 def body(freqs, receivers, data, block_of_slot, receiver_order):
@@ -303,6 +323,7 @@
             pltpu.SemaphoreType.DMA((freqs,)),
             pltpu.SemaphoreType.DMA((freqs,)),
             pltpu.SemaphoreType.DMA((2,)),
+            pltpu.SemaphoreType.REGULAR((3,)),
         ],
         compiler_params=pltpu.CompilerParams(
             collective_id=0, has_side_effects=True, vmem_limit_bytes=60 * 2**20
@@ -320,12 +341,12 @@
     traces = pl.pallas_call(
         transform_kernel,
         out_shape=jax.ShapeDtypeStruct((groups, each, width, NT), jnp.bfloat16),
-        grid=(each,),
+        grid=(2,),
         in_specs=[
             pl.BlockSpec(moved.shape, lambda i: (0, 0)),
             pl.BlockSpec(table.shape, lambda i: (0, 0)),
         ],
-        out_specs=pl.BlockSpec((groups, 1, width, NT), lambda i: (0, i, 0, 0)),
+        out_specs=pl.BlockSpec((groups, each // 2, width, NT), lambda i: (0, i, 0, 0)),
         name="transform",
     )(moved, table)
     return traces.reshape(part, width, NT)

time: 53.2 us -> 51.1 us (0.961); the launches traced: 52.3 us -> 51 us
  Pallas kernels: 52.3 us -> 51 us
    pallas_call x1, Pallas kernels: 4.96 us -> 2.83 us  [body(): pl.pallas_call(transform_kernel, out_shape=jax.ShapeDtypeStruct((groups,...]
    pallas_call x1, Pallas kernels: 47.4 us -> 48.1 us  [body(): pl.pallas_call(functools.partial(gather_kernel, freqs), out_shape=jax.Sha...]
where the time goes in v3:
time: 51.1 us; the launch traced here: 51 us
  Pallas kernels  51 us (100%)
    pallas_call x1, Pallas kernels, body(): pl.pallas_call(functools.partial(gather_kernel, freqs), out_shape=jax.Sha...  48.1 us
    pallas_call x1, Pallas kernels, body(): pl.pallas_call(transform_kernel, out_shape=jax.ShapeDtypeStruct((groups,...  2.83 us

profile of v3, /device:TPU:0, one launch (start us, length us, event | category | flops | bytes accessed | tf_op | source)
XLA Modules:
  0.0 51.0 jit_solution(18055149200195390643)
XLA Ops:
  0.0 48.1 %gather_multiply_exchange.1.spectra_ref = bf16[512,128]{1,0:T(8,128)(2,1)} custom-call(s32[16]{0:T(128)} %block_ref.1, s32[1,256]{1,0:T(1,128)} %bitcast.6, bf16[512,512]{1,0:T(8,128)(2,1)} %bitcast.5, bf16[2,16,512,128]{3,2,1,0:T(8,128)(2,1)} %bitcast.4), custom_call_target="tpu_custom_call" | custom-call | tf_op jit(solution)/shard_map/gather_multiply_exchange/pallas_call | solution.py:303
  48.1 2.8 %transform.1 = bf16[4,8,128,256]{3,2,1,0:T(8,128)(2,1)} custom-call(bf16[512,128]{1,0:T(8,128)(2,1)} %gather_multiply_exchange.1.spectra_ref, f32[32,256]{1,0:T(8,128)} %constant.2.clone.table_ref), custom_call_target="tpu_custom_call" | custom-call | tf_op jit(solution)/shard_map/transform/pallas_call | solution.py:341

commit v4 on v3

--- a/solution.py
+++ b/solution.py
@@ -12,24 +12,20 @@
 NT = 256
 MESH = pl.DeviceIdType.MESH
 CHUNK = 64
-
+PLACES = [(2, 1), (1, 1), (3, 1), (2, 0), (0, 1), (1, 0), (3, 0), (0, 0)]
+
+LOW, HIGH, EDGE = (0, 256), (256, 256), 80
+AROUND = [(0, 1, EDGE, 2 * CHUNK - EDGE)] + [(0, 1, p * CHUNK, CHUNK) for p in range(2, 8)]
 SENDS = {
-    "xp": [(0, 0, 0, 4), (0, 0, 4, 4)]
-    + [(-1, 0, k, 1) for k in range(4)]
-    + [(0, 1, 1, 3), (0, 1, 4, 2), (0, 1, 6, 2)],
-    "xm": [(0, 0, 4, 4), (0, 0, 0, 4)]
-    + [(1, 0, 4 + k, 1) for k in range(4)]
-    + [(0, 1, 4, 3), (0, 1, 2, 2), (0, 1, 0, 2)],
-    "z": [(0, 0, 0, 4), (0, 0, 4, 4), (-1, 0, 0, 1), (1, 0, 7, 1)]
-    + [(2, 0, 4 * (k % 2) + k // 2, 1) for k in range(8)],
-    "c": [(0, 0, 0, 4), (0, 0, 4, 4)]
-    + [(-1, 0, 0, 4), (1, 0, 4, 4), (0, 1, 0, 4)]
-    + [(-1, 0, 4, 4), (1, 0, 0, 4), (0, 1, 4, 4)]
-    + [(2, 0, 0, 4), (2, 0, 4, 4)]
-    + [(-1, 1, 0, 4), (1, 1, 4, 4), (2, 1, 0, 2), (2, 1, 4, 2)]
-    + [(-1, 1, 4, 2), (1, 1, 2, 2)]
-    + [(2, 1, 2, 2), (2, 1, 6, 2)]
-    + [(-1, 1, 6, 2), (1, 1, 0, 2)],
+    "xp": [(0, 0, *LOW), (0, 0, *HIGH)] + [(-1, 0, k * CHUNK, CHUNK) for k in range(4)] + AROUND,
+    "xm": [(0, 0, *HIGH), (0, 0, *LOW)] + [(1, 0, k * CHUNK, CHUNK) for k in range(4, 8)] + AROUND,
+    "z": [(0, 0, *LOW), (0, 0, *HIGH), (-1, 0, 0, EDGE), (1, 0, 0, EDGE)]
+    + [(2, 0, p * CHUNK, CHUNK) for p in range(8)],
+    "c": [(0, 0, *LOW), (0, 0, *HIGH)]
+    + [(-1, 0, *LOW), (1, 0, *HIGH), (0, 1, *LOW)]
+    + [(-1, 0, *HIGH), (1, 0, *LOW), (0, 1, *HIGH)]
+    + [(2, 0, *LOW), (2, 0, *HIGH)]
+    + [(dx, 1, p * CHUNK, CHUNK) for p in range(8) for dx in (-1, 1, 2)],
 }
 SHIFT = {"xp": (-1, 0, 0), "xm": (1, 0, 0), "z": (0, 1, 0), "c": (0, 0, 1)}
 COUNT = {link: len(rows) for link, rows in SENDS.items()}
@@ -48,7 +44,7 @@
 
 def gather_kernel(
     freqs, block_ref, order_ref, own_hbm, data_hbm, out_ref,
-    held, data, acc, perm, mix, outgoing, arrived,
+    held, data, raw, acc, perm, mix, outgoing, arrived,
     sx, rx, sf, rf, local, known,
 ):
     me = lax.axis_index("src")
@@ -68,7 +64,11 @@
         first[link] = at
         at += COUNT[link]
 
-    own_copy = pltpu.make_async_copy(own_hbm, held.at[me], local.at[0])
+    def place(p, sign=1):
+        dy, dz = PLACES[p]
+        return ((mine // 2 + sign * dy + 4) % 4) * 2 + (mine % 2 + dz) % 2
+
+    own_copy = pltpu.make_async_copy(own_hbm, raw, local.at[0])
     data_copy = pltpu.make_async_copy(data_hbm, data, local.at[1])
     own_copy.start()
     data_copy.start()
@@ -80,6 +80,18 @@
     inner, outer = {"src": target["z"]}, {"src": target["z"], "freq": mine + 1 - 2 * (mine % 2)}
     for peer in (after, before, outer):
         pl.semaphore_signal(barrier, inc=1, device_id=peer, device_id_type=MESH)
+
+    ids = lax.broadcasted_iota(jnp.int32, (rows, rows), 0)
+    chosen = jnp.where(ids == order_ref[...], 1.0, 0.0).astype(jnp.float32)
+    perm[...] = chosen.T.astype(jnp.bfloat16)
+    picks = jnp.concatenate(
+        [perm[pl.ds(pl.multiple_of(place(p) * part, part), part), :] for p in range(freqs)], 0
+    )
+    own_copy.wait()
+    for ri in range(2):
+        sorted_rows = jnp.dot(picks, raw[ri * rows : (ri + 1) * rows, :], preferred_element_type=jnp.float32)
+        for p in range(freqs):
+            held[me, pl.ds(p * CHUNK + ri * part, part), :] = sorted_rows[p * part : (p + 1) * part].astype(jnp.bfloat16)
     pl.semaphore_wait(barrier, len(SENDS) + 3)
 
     rounds = ((before, inner), (before, after), (before,))
@@ -97,7 +109,7 @@
         if received:
             sx_, sz_, dc = SHIFT[link]
             dx, dz = dx + sx_, dz + sz_
-        piece = held.at[slot(dx, dz, dc), pl.ds(low * CHUNK, count * CHUNK)]
+        piece = held.at[slot(dx, dz, dc), pl.ds(low, count)]
         return pltpu.make_async_remote_copy(
             src_ref=piece,
             dst_ref=piece,
@@ -119,14 +131,31 @@
         j = slot(dx, dz, dc)
         block = block_ref[j]
         right = jnp.concatenate([data[0, block], data[1, block]], 1)
-        span = pl.ds(low * CHUNK, count * CHUNK)
+        span = pl.ds(low, count)
         value = jnp.dot(held[j, span, :], right, preferred_element_type=jnp.float32)
         if fresh:
             acc[span, :] = value
         else:
             acc[span, :] += value
 
-    own_copy.wait()
+    def finish(p):
+        mid, half = p * CHUNK + part, acc.shape[1] // 2
+        top, low = acc[p * CHUNK : mid, :], acc[mid : mid + part, :]
+        real = top[:, :half] - low[:, half:]
+        imag = top[:, half:] + low[:, :half]
+        return jnp.concatenate([real, imag], 1).astype(jnp.bfloat16)
+
+    def share(p, received=False):
+        landing = place(p, -1) if received else mine
+        return pltpu.make_async_remote_copy(
+            src_ref=outgoing.at[pl.ds(p * part, part)],
+            dst_ref=arrived.at[pl.ds(pl.multiple_of(landing * part, part), part)],
+            send_sem=sf.at[p],
+            recv_sem=rf.at[p],
+            device_id={"freq": place(p)},
+            device_id_type=MESH,
+        )
+
     send("xp", 0)
     send("xm", 0)
     send("z", 0)
@@ -136,18 +165,15 @@
     send("c", 0, 1)
     tell(0)
 
-    ids = lax.broadcasted_iota(jnp.int32, (rows, rows), 0)
-    chosen = jnp.where(ids == order_ref[...], 1.0, 0.0).astype(jnp.float32)
-    perm[...] = chosen.T.astype(jnp.bfloat16)
     n = lax.broadcasted_iota(jnp.int32, (2 * rows, 1), 0)
     source = (n % 2) * rows + ((n // 2) % freqs) * part + n // (2 * freqs)
     m = lax.broadcasted_iota(jnp.int32, (2 * rows, 2 * rows), 1)
     mix[...] = jnp.where(m == source, 1.0, 0.0).astype(jnp.bfloat16)
 
     data_copy.wait()
-    product(0, 0, 0, 0, 8, fresh=True)
+    product(0, 0, 0, 0, 2 * rows, fresh=True)
     wait("c", 0, 1)
-    product(0, 0, 1, 0, 8)
+    product(0, 0, 1, 0, 2 * rows)
 
     wait("xp", 0)
     send("xp", 2, 3, 4, 5)
@@ -155,127 +181,90 @@
     send("c", 2)
     wait("xm", 0)
     send("xm", 2, 3, 4, 5)
-    send("z", 3)
     send("c", 3)
     wait("z", 0)
     send("c", 4)
-    product(-1, 0, 0, 0, 4)
-    product(1, 0, 0, 4, 4)
-    product(0, 1, 0, 0, 4)
+    product(-1, 0, 0, *LOW)
+    product(1, 0, 0, *HIGH)
+    product(0, 1, 0, *LOW)
     hear(0)
     tell(1)
     wait("c", 2, 3, 4)
-    product(-1, 0, 1, 0, 4)
-    product(1, 0, 1, 4, 4)
-    product(0, 1, 1, 0, 4)
-
+    product(-1, 0, 1, *LOW)
+    product(1, 0, 1, *HIGH)
+    product(0, 1, 1, *LOW)
+
+    wait("xm", 1)
+    send("z", 3)
     wait("z", 1)
-    send("xp", 6, 7, 8)
-    send("xm", 6, 7, 8)
+    send("xp", *range(6, 13))
+    send("xm", *range(6, 13))
     wait("xp", 1)
-    send("c", 5)
-    wait("xm", 1)
-    send("c", 6, 7)
-    product(-1, 0, 0, 4, 4)
-    product(1, 0, 0, 0, 4)
-    product(0, 1, 0, 4, 4)
+    send("c", 5, 6, 7)
+    product(-1, 0, 0, *HIGH)
+    product(1, 0, 0, *LOW)
+    product(0, 1, 0, *HIGH)
     hear(1)
     tell(2)
     wait("c", 5, 6, 7)
     hear(2)
-    product(-1, 0, 1, 4, 4)
-    product(1, 0, 1, 0, 4)
-    product(0, 1, 1, 4, 4)
 
     for k in range(4):
         wait("xp", 2 + k)
-        send("z", 4 + 2 * k)
+        send("z", 4 + k)
+        if k == 0:
+            product(-1, 0, 1, *HIGH)
+            product(1, 0, 1, *LOW)
+            product(0, 1, 1, *HIGH)
+    send("c", 8)
+    for k in range(4):
         wait("xm", 2 + k)
-        send("z", 5 + 2 * k)
-    send("c", 8, 9)
-    product(2, 0, 0, 0, 8)
+        send("z", 8 + k)
+    send("c", 9)
+    product(2, 0, 0, 0, 2 * rows)
     wait("c", 8, 9)
-    product(2, 0, 1, 0, 8)
-
-    wait("z", 2, 3)
-    wait("xp", 6)
-    send("c", 10)
-    wait("xm", 6)
-    send("c", 11)
-    wait("z", 4, 5, 6, 7)
-    send("c", 12, 13)
-    product(-1, 1, 0, 0, 4)
-    product(1, 1, 0, 4, 4)
-    wait("c", 10, 11)
-    product(-1, 1, 1, 0, 4)
-    product(1, 1, 1, 4, 4)
-
-    wait("xp", 7)
-    send("c", 14)
-    wait("xm", 7)
-    send("c", 15)
-    product(-1, 1, 0, 4, 2)
-    product(1, 1, 0, 2, 2)
-    wait("z", 8, 10)
-    send("c", 16)
-    wait("z", 9, 11)
-    send("c", 17)
-    product(2, 1, 0, 0, 8)
-    wait("c", 14, 15)
-    product(-1, 1, 1, 4, 2)
-    product(1, 1, 1, 2, 2)
-    wait("c", 12, 13, 16, 17)
-    product(2, 1, 1, 0, 8)
-
-    wait("xp", 8)
-    send("c", 18)
-    wait("xm", 8)
-    send("c", 19)
-    product(-1, 1, 0, 6, 2)
-    product(1, 1, 0, 0, 2)
-    wait("c", 18, 19)
-    product(-1, 1, 1, 6, 2)
-    product(1, 1, 1, 0, 2)
-
-    half = acc.shape[1] // 2
-    real = acc[:rows, :half] - acc[rows:, half:]
-    imag = acc[:rows, half:] + acc[rows:, :half]
-    spectra = jnp.concatenate([real, imag], 1).astype(jnp.bfloat16)
-    outgoing[...] = jnp.dot(perm[...], spectra, preferred_element_type=jnp.float32).astype(jnp.bfloat16)
-
-    def share(d, received=False):
-        peer = (mine + d) % freqs
-        back = (mine - d + freqs) % freqs
-        taken = outgoing.at[pl.ds(pl.multiple_of(peer * part, part), part)]
-        landing = back if received else mine
-        return pltpu.make_async_remote_copy(
-            src_ref=taken,
-            dst_ref=arrived.at[pl.ds(pl.multiple_of(landing * part, part), part)],
-            send_sem=sf.at[d],
-            recv_sem=rf.at[d],
-            device_id={"freq": peer},
-            device_id_type=MESH,
-        )
-
-    for d in range(1, freqs):
-        share(d).start()
+    product(2, 0, 1, 0, 2 * rows)
+
     here = pl.ds(pl.multiple_of(mine * part, part), part)
-    keep = pltpu.make_async_copy(outgoing.at[here], arrived.at[here], local.at[0])
-    keep.start()
+    for p in range(freqs + 1):
+        if p < freqs:
+            if p == 0:
+                wait("z", 2, 3)
+            else:
+                wait("xp", 5 + p)
+                send("c", 10 + 3 * p)
+                wait("xm", 5 + p)
+                send("c", 11 + 3 * p)
+            if p == 0:
+                send("c", 10, 11)
+            wait("z", 4 + p)
+            send("c", 12 + 3 * p)
+            for dx in (-1, 1, 2):
+                product(dx, 1, 0, p * CHUNK, CHUNK)
+        if p > 0:
+            last = p - 1
+            for k, dx in enumerate((-1, 1, 2)):
+                wait("c", 10 + 3 * last + k)
+                product(dx, 1, 1, last * CHUNK, CHUNK)
+            if last < freqs - 1:
+                outgoing[pl.ds(last * part, part), :] = finish(last)
+                share(last).start()
+            else:
+                arrived[here, :] = finish(last)
     for link in SENDS:
         for k in range(COUNT[link]):
             copy(link, k).wait_send()
-    keep.wait()
-    for d in range(1, freqs):
-        share(d, True).wait_recv()
-
+    for p in range(freqs - 1):
+        share(p, True).wait_recv()
+
+    half = acc.shape[1] // 2
     stacked = jnp.concatenate([arrived[:, :half], arrived[:, half:]], 0)
     mixed = jnp.dot(mix[...], stacked, preferred_element_type=jnp.float32)
     for g in range(2 * rows // half):
         span = pl.ds(g * half, half)
         out_ref[span, :] = mixed[g * half : (g + 1) * half, :].T.astype(jnp.bfloat16)
-    for d in range(1, freqs):
-        share(d).wait_send()
+    for p in range(freqs - 1):
+        share(p).wait_send()
 
 
 def transform_kernel(spectra_ref, table_ref, out_ref):
@@ -313,6 +302,7 @@
         scratch_shapes=[
             pltpu.VMEM((slots, 2 * rows, depth), jnp.bfloat16),
             pltpu.VMEM((2, slots, depth, width), jnp.bfloat16),
+            pltpu.VMEM((2 * rows, depth), jnp.bfloat16),
             pltpu.VMEM((2 * rows, 2 * width), jnp.float32),
             pltpu.VMEM((rows, rows), jnp.bfloat16),
             pltpu.VMEM((2 * rows, 2 * rows), jnp.bfloat16),

time: 51.1 us -> 45.6 us (0.89)
  Pallas kernels: 51 us -> 45.2 us
    pallas_call x1, Pallas kernels: 48.1 us -> 42.4 us  [body(): pl.pallas_call(functools.partial(gather_kernel, freqs), out_shape=jax.Sha...]
where the time goes in v4:
time: 45.6 us; the launch traced here: 45.2 us
  Pallas kernels  45.2 us (99%)
    pallas_call x1, Pallas kernels, body(): pl.pallas_call(functools.partial(gather_kernel, freqs), out_shape=jax.Sha...  42.4 us
    pallas_call x1, Pallas kernels, body(): pl.pallas_call(transform_kernel, out_shape=jax.ShapeDtypeStruct((groups,...  2.83 us

profile of v4, /device:TPU:0, one launch (start us, length us, event | category | flops | bytes accessed | tf_op | source)
XLA Modules:
  0.0 45.2 jit_solution(2041159675495425656)
XLA Ops:
  0.0 42.4 %gather_multiply_exchange.1.spectra_ref = bf16[512,128]{1,0:T(8,128)(2,1)} custom-call(s32[16]{0:T(128)} %block_ref.1, s32[1,256]{1,0:T(1,128)} %bitcast.6, bf16[512,512]{1,0:T(8,128)(2,1)} %bitcast.5, bf16[2,16,512,128]{3,2,1,0:T(8,128)(2,1)} %bitcast.4), custom_call_target="tpu_custom_call" | custom-call | tf_op jit(solution)/shard_map/gather_multiply_exchange/pallas_call | solution.py:292
  42.4 2.8 %transform.1 = bf16[4,8,128,256]{3,2,1,0:T(8,128)(2,1)} custom-call(bf16[512,128]{1,0:T(8,128)(2,1)} %gather_multiply_exchange.1.spectra_ref, f32[32,256]{1,0:T(8,128)} %constant.2.clone.table_ref), custom_call_target="tpu_custom_call" | custom-call | tf_op jit(solution)/shard_map/transform/pallas_call | solution.py:331

commit v5 on v4

--- a/solution.py
+++ b/solution.py
@@ -43,8 +43,8 @@
 
 
 def gather_kernel(
-    freqs, block_ref, order_ref, own_hbm, data_hbm, out_ref,
-    held, data, raw, acc, perm, mix, outgoing, arrived,
+    freqs, block_hbm, order_hbm, own_hbm, data_hbm, out_ref,
+    block_ref, order_ref, held, data, raw, acc, perm, mix, outgoing, arrived,
     sx, rx, sf, rf, local, known,
 ):
     me = lax.axis_index("src")
@@ -68,11 +68,6 @@
         dy, dz = PLACES[p]
         return ((mine // 2 + sign * dy + 4) % 4) * 2 + (mine % 2 + dz) % 2
 
-    own_copy = pltpu.make_async_copy(own_hbm, raw, local.at[0])
-    data_copy = pltpu.make_async_copy(data_hbm, data, local.at[1])
-    own_copy.start()
-    data_copy.start()
-
     barrier = pltpu.get_barrier_semaphore()
     for link in SENDS:
         pl.semaphore_signal(barrier, inc=1, device_id={"src": target[link]}, device_id_type=MESH)
@@ -81,7 +76,15 @@
     for peer in (after, before, outer):
         pl.semaphore_signal(barrier, inc=1, device_id=peer, device_id_type=MESH)
 
+    order_copy = pltpu.make_async_copy(order_hbm, order_ref, local.at[2])
+    own_copy = pltpu.make_async_copy(own_hbm, raw, local.at[0])
+    block_copy = pltpu.make_async_copy(block_hbm, block_ref, local.at[3])
+    data_copy = pltpu.make_async_copy(data_hbm, data, local.at[1])
+    for one in (order_copy, own_copy, block_copy, data_copy):
+        one.start()
+
     ids = lax.broadcasted_iota(jnp.int32, (rows, rows), 0)
+    order_copy.wait()
     chosen = jnp.where(ids == order_ref[...], 1.0, 0.0).astype(jnp.float32)
     perm[...] = chosen.T.astype(jnp.bfloat16)
     picks = jnp.concatenate(
@@ -170,6 +173,7 @@
     m = lax.broadcasted_iota(jnp.int32, (2 * rows, 2 * rows), 1)
     mix[...] = jnp.where(m == source, 1.0, 0.0).astype(jnp.bfloat16)
 
+    block_copy.wait()
     data_copy.wait()
     product(0, 0, 0, 0, 2 * rows, fresh=True)
     wait("c", 0, 1)
@@ -267,20 +271,23 @@
         share(p).wait_send()
 
 
-def transform_kernel(spectra_ref, table_ref, out_ref):
+def transform_kernel(spectra_ref, table_ref, out_hbm, done, sems):
     coefs = table_ref.shape[0] // 2
-    each = spectra_ref.shape[1] // coefs
-    groups, count, width, times = out_ref.shape
-    step = pl.program_id(0)
+    each, groups, width, times = done.shape
     high, low = table_ref[:coefs, :], table_ref[coefs:, :]
     full = jnp.concatenate([high] * each + [low] * each, 0)
     row = lax.broadcasted_iota(jnp.int32, full.shape, 0)
     left = jnp.concatenate([spectra_ref[...], spectra_ref[...]], 1)
-    for u in range(count):
-        here = (row // coefs) % each == step * count + u
+    copies = []
+    for u in range(each):
+        here = (row // coefs) % each == u
         right = jnp.where(here, full, 0.0).astype(jnp.bfloat16)
         value = jnp.dot(left, right, preferred_element_type=jnp.float32)
-        out_ref[:, u] = value.astype(jnp.bfloat16).reshape(groups, width, times)
+        done[u] = value.astype(jnp.bfloat16).reshape(groups, width, times)
+        copies.append(pltpu.make_async_copy(done.at[u], out_hbm.at[:, u], sems.at[u]))
+        copies[-1].start()
+    for one in copies:
+        one.wait()
 
 
 def body(freqs, receivers, data, block_of_slot, receiver_order):
@@ -293,13 +300,15 @@
         functools.partial(gather_kernel, freqs),
         out_shape=jax.ShapeDtypeStruct((2 * rows, width), jnp.bfloat16),
         in_specs=[
-            pl.BlockSpec(memory_space=pltpu.SMEM),
-            pl.BlockSpec(memory_space=pltpu.VMEM),
+            pl.BlockSpec(memory_space=pl.ANY),
+            pl.BlockSpec(memory_space=pl.ANY),
             pl.BlockSpec(memory_space=pl.ANY),
             pl.BlockSpec(memory_space=pl.ANY),
         ],
         out_specs=pl.BlockSpec(memory_space=pltpu.VMEM),
         scratch_shapes=[
+            pltpu.SMEM((slots,), jnp.int32),
+            pltpu.VMEM((1, rows), jnp.int32),
             pltpu.VMEM((slots, 2 * rows, depth), jnp.bfloat16),
             pltpu.VMEM((2, slots, depth, width), jnp.bfloat16),
             pltpu.VMEM((2 * rows, depth), jnp.bfloat16),
@@ -312,7 +321,7 @@
             pltpu.SemaphoreType.DMA((copies,)),
             pltpu.SemaphoreType.DMA((freqs,)),
             pltpu.SemaphoreType.DMA((freqs,)),
-            pltpu.SemaphoreType.DMA((2,)),
+            pltpu.SemaphoreType.DMA((4,)),
             pltpu.SemaphoreType.REGULAR((3,)),
         ],
         compiler_params=pltpu.CompilerParams(
@@ -331,12 +340,12 @@
     traces = pl.pallas_call(
         transform_kernel,
         out_shape=jax.ShapeDtypeStruct((groups, each, width, NT), jnp.bfloat16),
-        grid=(2,),
-        in_specs=[
-            pl.BlockSpec(moved.shape, lambda i: (0, 0)),
-            pl.BlockSpec(table.shape, lambda i: (0, 0)),
+        in_specs=[pl.BlockSpec(memory_space=pltpu.VMEM)] * 2,
+        out_specs=pl.BlockSpec(memory_space=pl.ANY),
+        scratch_shapes=[
+            pltpu.VMEM((each, groups, width, NT), jnp.bfloat16),
+            pltpu.SemaphoreType.DMA((each,)),
         ],
-        out_specs=pl.BlockSpec((groups, each // 2, width, NT), lambda i: (0, i, 0, 0)),
         name="transform",
     )(moved, table)
     return traces.reshape(part, width, NT)

time: 45.6 us -> 44.5 us (0.976)
  Pallas kernels: 45.2 us -> 44.2 us
    pallas_call x1, Pallas kernels: 42.4 us -> 41.6 us  [body(): pl.pallas_call(functools.partial(gather_kernel, freqs), out_shape=jax.Sha...]
where the time goes in v5:
time: 44.5 us; the launch traced here: 44.2 us
  Pallas kernels  44.2 us (99%)
    pallas_call x1, Pallas kernels, body(): pl.pallas_call(functools.partial(gather_kernel, freqs), out_shape=jax.Sha...  41.6 us
    pallas_call x1, Pallas kernels, body(): pl.pallas_call(transform_kernel, out_shape=jax.ShapeDtypeStruct((groups,...  2.58 us

profile of v5, /device:TPU:0, one launch (start us, length us, event | category | flops | bytes accessed | tf_op | source)
XLA Modules:
  0.0 44.2 jit_solution(10434164532218663469)
XLA Ops:
  0.0 41.6 %gather_multiply_exchange.1.spectra_ref = bf16[512,128]{1,0:T(8,128)(2,1)} custom-call(s32[16]{0:T(128)} %block_hbm.1, s32[1,256]{1,0:T(1,128)} %bitcast.6, bf16[512,512]{1,0:T(8,128)(2,1)} %bitcast.5, bf16[2,16,512,128]{3,2,1,0:T(8,128)(2,1)} %bitcast.4), custom_call_target="tpu_custom_call" | custom-call | tf_op jit(solution)/shard_map/gather_multiply_exchange/pallas_call | solution.py:299
  41.6 2.6 %transform.1 = bf16[4,8,128,256]{3,2,1,0:T(8,128)(2,1)} custom-call(bf16[512,128]{1,0:T(8,128)(2,1)} %gather_multiply_exchange.1.spectra_ref, f32[32,256]{1,0:T(8,128)} %constant.2.clone.table_ref), custom_call_target="tpu_custom_call" | custom-call | tf_op jit(solution)/shard_map/transform/pallas_call | solution.py:340

commit v6 on v5

--- a/solution.py
+++ b/solution.py
@@ -12,18 +12,39 @@
 NT = 256
 MESH = pl.DeviceIdType.MESH
 CHUNK = 64
-PLACES = [(2, 1), (1, 1), (3, 1), (2, 0), (0, 1), (1, 0), (3, 0), (0, 0)]
+
+
+def sending_order(y_size, halves):
+    def late(f):
+        return 0.8 * (f // halves) + 2.2 * (f % halves)
+
+    def need(f, q):
+        dy = abs(f // halves - q // halves)
+        hops = min(dy, y_size - dy) + 2 * (f % halves != q % halves)
+        return 0.75 * hops + late(f) - late(q)
+
+    count = y_size * halves
+    return [sorted((q for q in range(count) if q != f), key=lambda q: -need(f, q)) + [f] for f in range(count)]
+
+
+ORDER = sending_order(4, 2)
 
 LOW, HIGH, EDGE = (0, 256), (256, 256), 80
 AROUND = [(0, 1, EDGE, 2 * CHUNK - EDGE)] + [(0, 1, p * CHUNK, CHUNK) for p in range(2, 8)]
 SENDS = {
-    "xp": [(0, 0, *LOW), (0, 0, *HIGH)] + [(-1, 0, k * CHUNK, CHUNK) for k in range(4)] + AROUND,
-    "xm": [(0, 0, *HIGH), (0, 0, *LOW)] + [(1, 0, k * CHUNK, CHUNK) for k in range(4, 8)] + AROUND,
+    "xp": [(0, 0, *LOW), (0, 0, 256, 128)]
+    + [(-1, 0, k * CHUNK, CHUNK) for k in range(4)]
+    + [(0, 0, 384, 128)]
+    + AROUND,
+    "xm": [(0, 0, *LOW), (0, 0, *HIGH)]
+    + AROUND[:2]
+    + [(1, 0, k * CHUNK, CHUNK) for k in range(4, 8)]
+    + AROUND[2:],
     "z": [(0, 0, *LOW), (0, 0, *HIGH), (-1, 0, 0, EDGE), (1, 0, 0, EDGE)]
     + [(2, 0, p * CHUNK, CHUNK) for p in range(8)],
     "c": [(0, 0, *LOW), (0, 0, *HIGH)]
-    + [(-1, 0, *LOW), (1, 0, *HIGH), (0, 1, *LOW)]
-    + [(-1, 0, *HIGH), (1, 0, *LOW), (0, 1, *HIGH)]
+    + [(-1, 0, *LOW), (1, 0, *LOW), (0, 1, *LOW)]
+    + [(1, 0, *HIGH), (0, 1, *HIGH), (-1, 0, *HIGH)]
     + [(2, 0, *LOW), (2, 0, *HIGH)]
     + [(dx, 1, p * CHUNK, CHUNK) for p in range(8) for dx in (-1, 1, 2)],
 }
@@ -64,47 +85,52 @@
         first[link] = at
         at += COUNT[link]
 
-    def place(p, sign=1):
-        dy, dz = PLACES[p]
-        return ((mine // 2 + sign * dy + 4) % 4) * 2 + (mine % 2 + dz) % 2
+    def place(p):
+        if p == freqs - 1:
+            return mine
+        return sum(jnp.where(mine == f, ORDER[f][p], 0) for f in range(freqs))
+
+    farther = {"xp": x < 3, "xm": x == 0, "z": z == 0, "c": c == 1}
+    y, upper = mine // 2, mine % 2
+    below = [(y == 0, 2 + upper), (y == 0, 6 + upper), (y == 1, 4 + upper), (mine == 0, 1)]
+    above = jnp.where(y == 0, 0, jnp.where(y == 2, 2, 0) + upper)
+
+    def one(flag):
+        return jnp.where(flag, 1, 0)
+
+    def greet(semaphore, peer):
+        pl.semaphore_signal(semaphore, inc=1, device_id=peer, device_id_type=MESH)
 
     barrier = pltpu.get_barrier_semaphore()
     for link in SENDS:
-        pl.semaphore_signal(barrier, inc=1, device_id={"src": target[link]}, device_id_type=MESH)
-    after, before = {"freq": (mine + 2) % freqs}, {"freq": (mine + freqs - 2) % freqs}
-    inner, outer = {"src": target["z"]}, {"src": target["z"], "freq": mine + 1 - 2 * (mine % 2)}
-    for peer in (after, before, outer):
-        pl.semaphore_signal(barrier, inc=1, device_id=peer, device_id_type=MESH)
-
+        pl.when(farther[link])(functools.partial(greet, barrier, {"src": target[link]}))
+    for flag, peer in below:
+        pl.when(flag)(functools.partial(greet, barrier, {"freq": peer}))
     order_copy = pltpu.make_async_copy(order_hbm, order_ref, local.at[2])
     own_copy = pltpu.make_async_copy(own_hbm, raw, local.at[0])
     block_copy = pltpu.make_async_copy(block_hbm, block_ref, local.at[3])
     data_copy = pltpu.make_async_copy(data_hbm, data, local.at[1])
-    for one in (order_copy, own_copy, block_copy, data_copy):
-        one.start()
-
-    ids = lax.broadcasted_iota(jnp.int32, (rows, rows), 0)
-    order_copy.wait()
-    chosen = jnp.where(ids == order_ref[...], 1.0, 0.0).astype(jnp.float32)
-    perm[...] = chosen.T.astype(jnp.bfloat16)
-    picks = jnp.concatenate(
-        [perm[pl.ds(pl.multiple_of(place(p) * part, part), part), :] for p in range(freqs)], 0
-    )
-    own_copy.wait()
-    for ri in range(2):
-        sorted_rows = jnp.dot(picks, raw[ri * rows : (ri + 1) * rows, :], preferred_element_type=jnp.float32)
-        for p in range(freqs):
-            held[me, pl.ds(p * CHUNK + ri * part, part), :] = sorted_rows[p * part : (p + 1) * part].astype(jnp.bfloat16)
-    pl.semaphore_wait(barrier, len(SENDS) + 3)
-
-    rounds = ((before, inner), (before, after), (before,))
-
-    def tell(k):
-        for peer in rounds[k]:
-            pl.semaphore_signal(known.at[k], inc=1, device_id=peer, device_id_type=MESH)
-
-    def hear(k):
-        pl.semaphore_wait(known.at[k], len(rounds[k]))
+    for begun in (order_copy, own_copy, block_copy, data_copy):
+        begun.start()
+    nearer = sum(1 - one(farther[link]) for link in SENDS) + one(mine > 0)
+
+    def enter():
+        pl.semaphore_wait(barrier, nearer)
+
+    pl.when(nearer > 0)(enter)
+    for k, (link, far) in enumerate((("xp", "xm"), ("xm", "xp"), ("z", "z"), ("c", "c"))):
+        pl.when(jnp.logical_not(farther[far]))(functools.partial(greet, known.at[k], {"src": target[far]}))
+
+    peers_below = sum(one(flag) for flag, _ in below)
+
+    def report():
+        pl.when(peers_below > 0)(lambda: pl.semaphore_wait(known.at[4], peers_below))
+        pl.when(mine > 0)(functools.partial(greet, known.at[4], {"freq": above}))
+
+    def spread():
+        pl.when(mine > 0)(lambda: pl.semaphore_wait(known.at[5], 1))
+        for flag, peer in below:
+            pl.when(flag)(functools.partial(greet, known.at[5], {"freq": peer}))
 
     def copy(link, k, received=False):
         dx, dz, low, count = SENDS[link][k]
@@ -130,16 +156,15 @@
         for k in which:
             copy(link, k, True).wait_recv()
 
-    def product(dx, dz, dc, low, count, fresh=False):
-        j = slot(dx, dz, dc)
-        block = block_ref[j]
-        right = jnp.concatenate([data[0, block], data[1, block]], 1)
+    def product(blocks, low, count, fresh=False):
         span = pl.ds(low, count)
-        value = jnp.dot(held[j, span, :], right, preferred_element_type=jnp.float32)
-        if fresh:
-            acc[span, :] = value
-        else:
-            acc[span, :] += value
+        value = 0.0 if fresh else acc[span, :]
+        for dx, dz, dc in blocks:
+            j = slot(dx, dz, dc)
+            block = block_ref[j]
+            right = jnp.concatenate([data[0, block], data[1, block]], 1)
+            value += jnp.dot(held[j, span, :], right, preferred_element_type=jnp.float32)
+        acc[span, :] = value
 
     def finish(p):
         mid, half = p * CHUNK + part, acc.shape[1] // 2
@@ -148,25 +173,41 @@
         imag = top[:, half:] + low[:, :half]
         return jnp.concatenate([real, imag], 1).astype(jnp.bfloat16)
 
-    def share(p, received=False):
-        landing = place(p, -1) if received else mine
+    def share(p, sender=mine):
         return pltpu.make_async_remote_copy(
             src_ref=outgoing.at[pl.ds(p * part, part)],
-            dst_ref=arrived.at[pl.ds(pl.multiple_of(landing * part, part), part)],
+            dst_ref=arrived.at[pl.ds(pl.multiple_of(sender * part, part), part)],
             send_sem=sf.at[p],
-            recv_sem=rf.at[p],
+            recv_sem=rf.at[sender],
             device_id={"freq": place(p)},
             device_id_type=MESH,
         )
 
-    send("xp", 0)
-    send("xm", 0)
-    send("z", 0)
-    send("xp", 1)
-    send("xm", 1)
-    send("z", 1)
+    order_copy.wait()
+    ids = lax.broadcasted_iota(jnp.int32, (rows, rows), 0)
+    chosen = jnp.where(ids == order_ref[...], 1.0, 0.0).astype(jnp.float32)
+    perm[...] = chosen.T.astype(jnp.bfloat16)
+    own_copy.wait()
+    for side in range(2):
+        group = range(side * freqs // 2, (side + 1) * freqs // 2)
+        picks = jnp.concatenate(
+            [perm[pl.ds(pl.multiple_of(place(p) * part, part), part), :] for p in group], 0
+        )
+        for ri in range(2):
+            wide = jnp.dot(picks, raw[ri * rows : (ri + 1) * rows, :], preferred_element_type=jnp.float32)
+            for k, p in enumerate(group):
+                held[me, pl.ds(p * CHUNK + ri * part, part), :] = wide[k * part : (k + 1) * part].astype(jnp.bfloat16)
+    for near in (True, False):
+        for k, link in enumerate(("xp", "xm", "z")):
+
+            def begin(k=k, link=link, near=near):
+                if not near:
+                    pl.semaphore_wait(known.at[k], 1)
+                send(link, 0, 1)
+
+            pl.when(jnp.logical_not(farther[link]) if near else farther[link])(begin)
+    pl.when(farther["c"])(lambda: pl.semaphore_wait(known.at[3], 1))
     send("c", 0, 1)
-    tell(0)
 
     n = lax.broadcasted_iota(jnp.int32, (2 * rows, 1), 0)
     source = (n % 2) * rows + ((n // 2) % freqs) * part + n // (2 * freqs)
@@ -175,81 +216,72 @@
 
     block_copy.wait()
     data_copy.wait()
-    product(0, 0, 0, 0, 2 * rows, fresh=True)
+    product([(0, 0, 0)], 0, 2 * rows, fresh=True)
+
+    wait("xp", 0)
+    send("xp", 2, 3, 4, 5, 6)
+    send("z", 2)
+    wait("xm", 0)
+    send("z", 3)
+    wait("z", 0)
+    send("xm", 2, 3)
+    send("c", 2, 3, 4)
     wait("c", 0, 1)
-    product(0, 0, 1, 0, 2 * rows)
-
-    wait("xp", 0)
-    send("xp", 2, 3, 4, 5)
-    send("z", 2)
-    send("c", 2)
-    wait("xm", 0)
-    send("xm", 2, 3, 4, 5)
-    send("c", 3)
-    wait("z", 0)
-    send("c", 4)
-    product(-1, 0, 0, *LOW)
-    product(1, 0, 0, *HIGH)
-    product(0, 1, 0, *LOW)
-    hear(0)
-    tell(1)
+    product([(0, 0, 1)], 0, 2 * rows)
+    product([(-1, 0, 0), (1, 0, 0), (0, 1, 0)], *LOW)
+    report()
     wait("c", 2, 3, 4)
-    product(-1, 0, 1, *LOW)
-    product(1, 0, 1, *HIGH)
-    product(0, 1, 1, *LOW)
-
-    wait("xm", 1)
-    send("z", 3)
-    wait("z", 1)
-    send("xp", *range(6, 13))
-    send("xm", *range(6, 13))
-    wait("xp", 1)
-    send("c", 5, 6, 7)
-    product(-1, 0, 0, *HIGH)
-    product(1, 0, 0, *LOW)
-    product(0, 1, 0, *HIGH)
-    hear(1)
-    tell(2)
-    wait("c", 5, 6, 7)
-    hear(2)
-
-    for k in range(4):
+    product([(-1, 0, 1), (1, 0, 1), (0, 1, 1)], *LOW)
+
+    for k in range(2):
         wait("xp", 2 + k)
         send("z", 4 + k)
-        if k == 0:
-            product(-1, 0, 1, *HIGH)
-            product(1, 0, 1, *LOW)
-            product(0, 1, 1, *HIGH)
+    wait("xm", 1)
+    send("xm", 4, 5, 6, 7)
+    wait("z", 1)
+    send("xm", *range(8, 13))
+    send("xp", *range(7, 14))
+    send("c", 5, 6)
+    product([(1, 0, 0), (0, 1, 0)], *HIGH)
+    for k in range(2, 4):
+        wait("xp", 2 + k)
+        send("z", 4 + k)
     send("c", 8)
+    wait("c", 5, 6)
+    product([(1, 0, 1), (0, 1, 1)], *HIGH)
+    product([(2, 0, 0)], *LOW)
+    wait("xp", 1, 6)
+    send("c", 7)
+    product([(-1, 0, 0)], *HIGH)
+    spread()
     for k in range(4):
-        wait("xm", 2 + k)
+        wait("xm", 4 + k)
         send("z", 8 + k)
     send("c", 9)
-    product(2, 0, 0, 0, 2 * rows)
-    wait("c", 8, 9)
-    product(2, 0, 1, 0, 2 * rows)
-
+    product([(2, 0, 0)], *HIGH)
+    wait("c", 7, 8, 9)
+    product([(2, 0, 1)], *LOW)
+    product([(-1, 0, 1), (2, 0, 1)], *HIGH)
+
+    sides = (-1, 1, 2)
     here = pl.ds(pl.multiple_of(mine * part, part), part)
     for p in range(freqs + 1):
         if p < freqs:
             if p == 0:
                 wait("z", 2, 3)
+                send("c", 10, 11)
             else:
-                wait("xp", 5 + p)
+                wait("xp", 6 + p)
                 send("c", 10 + 3 * p)
-                wait("xm", 5 + p)
+                wait("xm", 1 + p if p < 3 else 5 + p)
                 send("c", 11 + 3 * p)
-            if p == 0:
-                send("c", 10, 11)
             wait("z", 4 + p)
             send("c", 12 + 3 * p)
-            for dx in (-1, 1, 2):
-                product(dx, 1, 0, p * CHUNK, CHUNK)
+            product([(dx, 1, 0) for dx in sides], p * CHUNK, CHUNK)
         if p > 0:
             last = p - 1
-            for k, dx in enumerate((-1, 1, 2)):
-                wait("c", 10 + 3 * last + k)
-                product(dx, 1, 1, last * CHUNK, CHUNK)
+            wait("c", *range(10 + 3 * last, 13 + 3 * last))
+            product([(dx, 1, 1) for dx in sides], last * CHUNK, CHUNK)
             if last < freqs - 1:
                 outgoing[pl.ds(last * part, part), :] = finish(last)
                 share(last).start()
@@ -259,7 +291,7 @@
         for k in range(COUNT[link]):
             copy(link, k).wait_send()
     for p in range(freqs - 1):
-        share(p, True).wait_recv()
+        share(p, (mine + 1 + p) % freqs).wait_recv()
 
     half = acc.shape[1] // 2
     stacked = jnp.concatenate([arrived[:, :half], arrived[:, half:]], 0)
@@ -322,7 +354,7 @@
             pltpu.SemaphoreType.DMA((freqs,)),
             pltpu.SemaphoreType.DMA((freqs,)),
             pltpu.SemaphoreType.DMA((4,)),
-            pltpu.SemaphoreType.REGULAR((3,)),
+            pltpu.SemaphoreType.REGULAR((6,)),
         ],
         compiler_params=pltpu.CompilerParams(
             collective_id=0, has_side_effects=True, vmem_limit_bytes=60 * 2**20

time: 44.5 us -> 42.6 us (0.957)
  Pallas kernels: 44.2 us -> 41.9 us
    pallas_call x1, Pallas kernels: 41.6 us -> 39.3 us  [body(): pl.pallas_call(functools.partial(gather_kernel, freqs), out_shape=jax.Sha...]
where the time goes in v6:
time: 42.6 us; the launch traced here: 41.9 us
  Pallas kernels  41.9 us (98%)
    pallas_call x1, Pallas kernels, body(): pl.pallas_call(functools.partial(gather_kernel, freqs), out_shape=jax.Sha...  39.3 us
    pallas_call x1, Pallas kernels, body(): pl.pallas_call(transform_kernel, out_shape=jax.ShapeDtypeStruct((groups,...  2.58 us

profile of v6, /device:TPU:0, one launch (start us, length us, event | category | flops | bytes accessed | tf_op | source)
XLA Modules:
  0.0 41.9 jit_solution(13462478400346509736)
XLA Ops:
  0.0 39.3 %gather_multiply_exchange.1.spectra_ref = bf16[512,128]{1,0:T(8,128)(2,1)} custom-call(s32[16]{0:T(128)} %block_hbm.1, s32[1,256]{1,0:T(1,128)} %bitcast.6, bf16[512,512]{1,0:T(8,128)(2,1)} %bitcast.5, bf16[2,16,512,128]{3,2,1,0:T(8,128)(2,1)} %bitcast.4), custom_call_target="tpu_custom_call" | custom-call | tf_op jit(solution)/shard_map/gather_multiply_exchange/pallas_call | solution.py:331
  39.3 2.6 %transform.1 = bf16[4,8,128,256]{3,2,1,0:T(8,128)(2,1)} custom-call(bf16[512,128]{1,0:T(8,128)(2,1)} %gather_multiply_exchange.1.spectra_ref, f32[32,256]{1,0:T(8,128)} %constant.2.clone.table_ref), custom_call_target="tpu_custom_call" | custom-call | tf_op jit(solution)/shard_map/transform/pallas_call | solution.py:372

commit v7 on v6

--- a/solution.py
+++ b/solution.py
@@ -156,10 +156,12 @@
         for k in which:
             copy(link, k, True).wait_recv()
 
-    def product(blocks, low, count, fresh=False):
+    def product(blocks, low, count, arriving=(), fresh=False):
         span = pl.ds(low, count)
         value = 0.0 if fresh else acc[span, :]
-        for dx, dz, dc in blocks:
+        for n, (dx, dz, dc) in enumerate(blocks):
+            if arriving:
+                wait("c", arriving[n])
             j = slot(dx, dz, dc)
             block = block_ref[j]
             right = jnp.concatenate([data[0, block], data[1, block]], 1)
@@ -270,23 +272,37 @@
             if p == 0:
                 wait("z", 2, 3)
                 send("c", 10, 11)
-            else:
+            wait("z", 4 + p)
+            send("c", 12 + 3 * p)
+            if p > 0:
                 wait("xp", 6 + p)
                 send("c", 10 + 3 * p)
                 wait("xm", 1 + p if p < 3 else 5 + p)
                 send("c", 11 + 3 * p)
-            wait("z", 4 + p)
-            send("c", 12 + 3 * p)
-            product([(dx, 1, 0) for dx in sides], p * CHUNK, CHUNK)
+            if p in (1, 3):
+                product([(dx, 1, 0) for dx in sides], (p - 1) * CHUNK, 2 * CHUNK)
+            elif p > 3:
+                product([(dx, 1, 0) for dx in sides], p * CHUNK, CHUNK)
         if p > 0:
             last = p - 1
-            wait("c", *range(10 + 3 * last, 13 + 3 * last))
-            product([(dx, 1, 1) for dx in sides], last * CHUNK, CHUNK)
-            if last < freqs - 1:
-                outgoing[pl.ds(last * part, part), :] = finish(last)
-                share(last).start()
-            else:
+            if last in (0, 2):
+                continue
+            pair = last in (1, 3)
+            if pair:
+                wait("c", *range(7 + 3 * last, 10 + 3 * last))
+            arrive = (2, 0, 1)
+            product(
+                [(sides[k], 1, 1) for k in arrive],
+                (last - pair) * CHUNK,
+                (1 + pair) * CHUNK,
+                [10 + 3 * last + k for k in arrive],
+            )
+            if last == freqs - 1:
                 arrived[here, :] = finish(last)
+                continue
+            for q in range(last - pair, last + 1):
+                outgoing[pl.ds(q * part, part), :] = finish(q)
+                share(q).start()
     for link in SENDS:
         for k in range(COUNT[link]):
             copy(link, k).wait_send()

time: 42.6 us -> 42.1 us (0.988)
  no operation moved by 1% of the time
where the time goes in v7:
time: 42.1 us; the launch traced here: 41.7 us
  Pallas kernels  41.7 us (99%)
    pallas_call x1, Pallas kernels, body(): pl.pallas_call(functools.partial(gather_kernel, freqs), out_shape=jax.Sha...  39.1 us
    pallas_call x1, Pallas kernels, body(): pl.pallas_call(transform_kernel, out_shape=jax.ShapeDtypeStruct((groups,...  2.58 us

profile of v7, /device:TPU:0, one launch (start us, length us, event | category | flops | bytes accessed | tf_op | source)
XLA Modules:
  0.0 41.7 jit_solution(15379935452370087197)
XLA Ops:
  0.0 39.1 %gather_multiply_exchange.1.spectra_ref = bf16[512,128]{1,0:T(8,128)(2,1)} custom-call(s32[16]{0:T(128)} %block_hbm.1, s32[1,256]{1,0:T(1,128)} %bitcast.6, bf16[512,512]{1,0:T(8,128)(2,1)} %bitcast.5, bf16[2,16,512,128]{3,2,1,0:T(8,128)(2,1)} %bitcast.4), custom_call_target="tpu_custom_call" | custom-call | tf_op jit(solution)/shard_map/gather_multiply_exchange/pallas_call | solution.py:347
  39.1 2.6 %transform.1 = bf16[4,8,128,256]{3,2,1,0:T(8,128)(2,1)} custom-call(bf16[512,128]{1,0:T(8,128)(2,1)} %gather_multiply_exchange.1.spectra_ref, f32[32,256]{1,0:T(8,128)} %constant.2.clone.table_ref), custom_call_target="tpu_custom_call" | custom-call | tf_op jit(solution)/shard_map/transform/pallas_call | solution.py:388

commit v8 on v7

--- a/solution.py
+++ b/solution.py
@@ -16,7 +16,7 @@
 
 def sending_order(y_size, halves):
     def late(f):
-        return 0.8 * (f // halves) + 2.2 * (f % halves)
+        return 0.4 * (f // halves) + 1.1 * (f % halves)
 
     def need(f, q):
         dy = abs(f // halves - q // halves)

time: 42.1 us -> 42.1 us (level)
  no operation moved by 1% of the time
where the time goes in v8:
time: 42.1 us; the launch traced here: 41.7 us
  Pallas kernels  41.7 us (99%)
    pallas_call x1, Pallas kernels, body(): pl.pallas_call(functools.partial(gather_kernel, freqs), out_shape=jax.Sha...  39.1 us
    pallas_call x1, Pallas kernels, body(): pl.pallas_call(transform_kernel, out_shape=jax.ShapeDtypeStruct((groups,...  2.58 us

profile of v8, /device:TPU:0, one launch (start us, length us, event | category | flops | bytes accessed | tf_op | source)
XLA Modules:
  0.0 41.7 jit_solution(5670950348997493244)
XLA Ops:
  0.0 39.1 %gather_multiply_exchange.1.spectra_ref = bf16[512,128]{1,0:T(8,128)(2,1)} custom-call(s32[16]{0:T(128)} %block_hbm.1, s32[1,256]{1,0:T(1,128)} %bitcast.6, bf16[512,512]{1,0:T(8,128)(2,1)} %bitcast.5, bf16[2,16,512,128]{3,2,1,0:T(8,128)(2,1)} %bitcast.4), custom_call_target="tpu_custom_call" | custom-call | tf_op jit(solution)/shard_map/gather_multiply_exchange/pallas_call | solution.py:347
  39.2 2.6 %transform.1 = bf16[4,8,128,256]{3,2,1,0:T(8,128)(2,1)} custom-call(bf16[512,128]{1,0:T(8,128)(2,1)} %gather_multiply_exchange.1.spectra_ref, f32[32,256]{1,0:T(8,128)} %constant.2.clone.table_ref), custom_call_target="tpu_custom_call" | custom-call | tf_op jit(solution)/shard_map/transform/pallas_call | solution.py:388
